TPU v7x, 256 devices: a whole 4x4x8 slice. The times are simulated.
256 devices in a mesh: src: 16 (over z_lo, y), rcv: 16 (over z_hi, x, core).
Axes of the slice: x: 4, y: 4, z: 8 (z_hi: 2, z_lo: 4; z = z_hi * 4 + z_lo), core: 2. Of those that a mesh axis runs over, the one named last changes fastest.
Arguments:
- records: bfloat16 [4096, 8192], P(('rcv', 'src')), may hold values from -6 to 6
- live_mask: int32 [4096], P(('rcv', 'src')), may hold values 0 or 1
- offsets: int32 [64], replicated, may hold values from 0 to 7936
- block_ids: int32 [2, 16], P(None, 'src'), may hold values from 0 to 31
Outputs:
- stacked: bfloat16 [2, 76, 2048, 4096], P(None, None, 'src', 'rcv')
All inputs are finite; a program needn't handle non-finite values. No bound on the sum of `live_mask` on one device may be relied on, other than what follows from the above.
Results may differ from a plain program's by a relative error of at most 0.0059.
Values may be sent and summed in bfloat16 or wider, within the bound.
A program may use at most 128 MiB of HBM per device.

v0:
```python
import jax
import jax.numpy as jnp
from jax import lax
from jax.sharding import PartitionSpec as P

L = 256
SB = 128
LAGS = 76


def broadcast(value, axis, source):
    kept = jnp.where(lax.axis_index(axis) == source, value, 0).astype(value.dtype)
    return lax.psum(kept, axis)


def build_tables(length, win_count, lag_count):
    sample_axis = jnp.arange(length, dtype=jnp.float32)
    bin_count = length // 2
    bin_axis = jnp.arange(bin_count, dtype=jnp.float32)
    phases = 2.0 * jnp.pi * sample_axis[:, None] * bin_axis[None, :] / length
    taper = 0.5 - 0.5 * jnp.cos(2.0 * jnp.pi * sample_axis / length)
    dft_table = jnp.concatenate(
        [taper[:, None] * jnp.cos(phases), -taper[:, None] * jnp.sin(phases)], axis=1
    ).astype(jnp.bfloat16)
    lag_axis = jnp.arange(lag_count, dtype=jnp.float32)
    weights = jnp.where(bin_axis == 0, 1.0, 2.0).astype(jnp.float32)
    lag_table = (
        weights[:, None]
        * jnp.cos(2.0 * jnp.pi * bin_axis[:, None] * lag_axis[None, :] / length)
        * (2.0 / (win_count * length))
    ).astype(jnp.bfloat16)
    return (dft_table, lag_table)


def transform(live_rec, offsets, dft_table):
    receiver_total = live_rec.shape[0]
    length = dft_table.shape[0]
    win_count = offsets.shape[0]
    windows = jax.vmap(lambda anchor: lax.dynamic_slice_in_dim(live_rec, anchor, length, 1))(
        offsets
    )
    flat_spec = jnp.dot(
        windows.reshape(win_count * receiver_total, length),
        dft_table,
        preferred_element_type=jnp.float32,
    ).astype(jnp.bfloat16)
    bin_count = dft_table.shape[1] // 2
    return (
        flat_spec.reshape(win_count, receiver_total, 2, bin_count)
        .transpose(3, 1, 2, 0)
        .reshape(bin_count, receiver_total, 2 * win_count)
    )


def correlate(source_block, receiver_block, lag_table, src_chan, rcv_chan):
    cross_spectrum = jnp.einsum(
        "mdt,mpt->mdp", source_block, receiver_block, preferred_element_type=jnp.float32
    ).astype(jnp.bfloat16)
    bin_count, src_count, receiver_total = cross_spectrum.shape
    mixed = jnp.dot(
        lag_table.T,
        cross_spectrum.reshape(bin_count, src_count * receiver_total),
        preferred_element_type=jnp.float32,
    )
    mixed = mixed.reshape(-1, src_count, receiver_total)
    self_pair = src_chan[:, None] == rcv_chan[None, :]
    return jnp.where(self_pair[None], 0.0, mixed).astype(jnp.bfloat16)


def local(records, live_mask, offsets, block_ids):
    group_member_count = records.shape[0] * lax.axis_size("src")
    dft_table, lag_table = build_tables(L, offsets.shape[0], LAGS)
    live_rec = records * live_mask[:, None].astype(records.dtype)
    local_spectrum = transform(live_rec, offsets, dft_table)
    receiver_block = lax.all_gather(local_spectrum, "src", axis=1, tiled=True)
    rcv_chan = lax.axis_index("rcv") * group_member_count + jnp.arange(
        group_member_count, dtype=jnp.int32
    )
    results = []
    for turn_index in range(block_ids.shape[0]):
        block_id = block_ids[turn_index, 0]
        first_chan = block_id * SB
        root_rank = first_chan // group_member_count
        beginning = first_chan % group_member_count
        portion = lax.dynamic_slice_in_dim(receiver_block, beginning, SB, 1)
        source_block = broadcast(portion, "rcv", root_rank)
        src_chan = first_chan + jnp.arange(SB, dtype=jnp.int32)
        results.append(correlate(source_block, receiver_block, lag_table, src_chan, rcv_chan))
    return jnp.stack(results)


def solution(mesh):
    in_specs = (P(("rcv", "src"), None), P(("rcv", "src")), P(), P(None, "src"))
    out_specs = P(None, None, "src", "rcv")
    return jax.shard_map(local, mesh=mesh, in_specs=in_specs, out_specs=out_specs, check_vma=False)
```

profile of v0, /device:TPU:1, one launch (start us, length us, event | category | flops | bytes accessed | tf_op | source)
XLA Modules:
  0.0 580.7 jit_solution(16682871106229429336)
XLA Ops:
  8.0 1.0 broadcast_multiply_fusion
  9.0 85.5 %while.1 = (s32[]{:T(128)}, bf16[16,8192]{1,0:T(8,128)(2,1)S(1)}, s32[64,2]{0,1:T(2,128)S(1)}, bf16[64,16,256]{2,1,0:T(8,128)(2,1)S(1)}, s32[]{:T(128)}) while((s32[]{:T(128)}, bf16[16,8192]{1,0:T(8,128)(2,1)S(1)}, s32[64,2]{0,1:T(2,128)S(1)}, bf16[64,16,256]{2,1,0:T(8,128)(2,1)S(1)}, s32[]{:T(128)}) %tuple.23), condition=%wide.while_cond, body=%wide.while_body.sunk | while | flops 2 | bytes 16481 | solution.py:39
  9.7 0.7 bitcast_dynamic-update-slice_fusion.2
  11.0 0.7 bitcast_dynamic-update-slice_fusion.2
  12.3 0.7 bitcast_dynamic-update-slice_fusion.2
  13.7 0.7 bitcast_dynamic-update-slice_fusion.2
  15.0 0.7 bitcast_dynamic-update-slice_fusion.2
  16.3 0.7 bitcast_dynamic-update-slice_fusion.2
  17.7 0.7 bitcast_dynamic-update-slice_fusion.2
  19.0 0.7 bitcast_dynamic-update-slice_fusion.2
  20.3 0.7 bitcast_dynamic-update-slice_fusion.2
  21.7 0.7 bitcast_dynamic-update-slice_fusion.2
  23.0 0.7 bitcast_dynamic-update-slice_fusion.2
  25.7 0.7 bitcast_dynamic-update-slice_fusion.2
  27.0 0.7 bitcast_dynamic-update-slice_fusion.2
  28.4 0.7 bitcast_dynamic-update-slice_fusion.2
  29.7 0.7 bitcast_dynamic-update-slice_fusion.2
  32.4 0.7 bitcast_dynamic-update-slice_fusion.2
  33.7 0.7 bitcast_dynamic-update-slice_fusion.2
  35.0 0.7 bitcast_dynamic-update-slice_fusion.2
  36.4 0.7 bitcast_dynamic-update-slice_fusion.2
  37.7 0.7 bitcast_dynamic-update-slice_fusion.2
  39.1 0.7 bitcast_dynamic-update-slice_fusion.2
  40.4 0.7 bitcast_dynamic-update-slice_fusion.2
  41.7 0.7 bitcast_dynamic-update-slice_fusion.2
  43.1 0.7 bitcast_dynamic-update-slice_fusion.2
  44.4 0.7 bitcast_dynamic-update-slice_fusion.2
  45.7 0.7 bitcast_dynamic-update-slice_fusion.2
  47.1 0.7 bitcast_dynamic-update-slice_fusion.2
  48.4 0.7 bitcast_dynamic-update-slice_fusion.2
  51.1 0.7 bitcast_dynamic-update-slice_fusion.2
  52.4 0.7 bitcast_dynamic-update-slice_fusion.2
  53.8 0.7 bitcast_dynamic-update-slice_fusion.2
  55.1 0.7 bitcast_dynamic-update-slice_fusion.2
  57.8 0.7 bitcast_dynamic-update-slice_fusion.2
  59.1 0.7 bitcast_dynamic-update-slice_fusion.2
  60.4 0.7 bitcast_dynamic-update-slice_fusion.2
  61.8 0.7 bitcast_dynamic-update-slice_fusion.2
  63.1 0.7 bitcast_dynamic-update-slice_fusion.2
  64.4 0.7 bitcast_dynamic-update-slice_fusion.2
  65.8 0.7 bitcast_dynamic-update-slice_fusion.2
  67.1 0.7 bitcast_dynamic-update-slice_fusion.2
  68.5 0.7 bitcast_dynamic-update-slice_fusion.2
  69.8 0.7 bitcast_dynamic-update-slice_fusion.2
  71.1 0.7 bitcast_dynamic-update-slice_fusion.2
  72.5 0.7 bitcast_dynamic-update-slice_fusion.2
  73.8 0.7 bitcast_dynamic-update-slice_fusion.2
  76.5 0.7 bitcast_dynamic-update-slice_fusion.2
  77.8 0.7 bitcast_dynamic-update-slice_fusion.2
  95.8 1.2 copy.10
  97.1 1.3 fusion.21
  99.6 122.5 %all-gather.2.cloned.1.call-done = bf16[128,256,128]{2,1,0:T(8,128)(2,1)} async-done(((bf16[128,16,128]{2,1,0:T(8,128)(2,1)}), bf16[128,256,128]{2,1,0:T(8,128)(2,1)}) %all-gather.2.cloned.1.call-update) | async-done | bytes 8388624 | tf_op jit(solution)/shard_map/all_gather | solution.py:75
  222.1 11.4 %dynamic-slice_select_fusion.1 = (bf16[128,128,128]{2,1,0:T(8,128)(2,1)}, bf16[128,128,128]{2,1,0:T(8,128)(2,1)}) fusion(bf16[128,256,128]{2,1,0:T(8,128)(2,1)} %all-gather.2.cloned.1.call-done, s32[]{:T(128)S(6)} %select_n.63, pred[]{:T(512)S(6)} %eq.58, s32[]{:T(128)S(6)} %select_n.69, pred[]{:T(512)S(6)} %eq.61), kind=kLoop, calls=%fused_computation.10 | loop fusion | flops 4194304 | bytes 16777226 | tf_op jit(solution)/shard_map/jit(_where)/select_n | solution.py:12
  233.7 236.2 %all-reduce.4.cloned.1.call-done = (bf16[128,128,128]{2,1,0:T(8,128)(2,1)}, bf16[128,128,128]{2,1,0:T(8,128)(2,1)}) async-done(((bf16[128,128,128]{2,1,0:T(8,128)(2,1)}, bf16[128,128,128]{2,1,0:T(8,128)(2,1)}), (bf16[128,128,128]{2,1,0:T(8,128)(2,1)}, bf16[128,128,128]{2,1,0:T(8,128)(2,1)})) %all-reduce.4.cloned.1.call-update) | async-done | bytes 8388624 | tf_op jit(solution)/shard_map/psum | solution.py:13
  469.9 10.4 %convolution_convert_fusion.1 = bf16[128,128,256]{2,1,0:T(8,128)(2,1)} fusion(bf16[128,128,128]{2,1,0:T(8,128)(2,1)} %get-tuple-element.22, bf16[128,256,128]{2,1,0:T(8,128)(2,1)} %all-gather.2.cloned.1.call-done), kind=kOutput, calls=%fused_computation.6 | convolution fusion | flops 1077936128 | bytes 20971520 | tf_op jit(solution)/shard_map/mdt,mpt->mdp/dot_general | solution.py:56
  480.3 12.5 %copy.14 = bf16[16,8,128,256]{3,1,2,0:T(8,128)(2,1)} copy(bf16[16,8,128,256]{3,2,1,0:T(8,128)(2,1)} %bitcast.43) | data formatting | bytes 16777216
  492.9 11.3 %copy.11 = bf16[32768,128]{1,0:T(8,128)(2,1)} copy(bf16[32768,128]{0,1:T(8,128)(2,1)} %bitcast.44) | data formatting | bytes 16777216 | tf_op jit(solution)/shard_map/dot_general | solution.py:60
  504.2 10.4 %convolution_convert_fusion = bf16[128,128,256]{2,1,0:T(8,128)(2,1)} fusion(bf16[128,128,128]{2,1,0:T(8,128)(2,1)} %get-tuple-element.21, bf16[128,256,128]{2,1,0:T(8,128)(2,1)} %all-gather.2.cloned.1.call-done), kind=kOutput, calls=%fused_computation.5 | convolution fusion | flops 1077936128 | bytes 20971520 | tf_op jit(solution)/shard_map/mdt,mpt->mdp/dot_general | solution.py:56
  514.6 12.3 %copy.15 = bf16[16,8,128,256]{3,1,2,0:T(8,128)(2,1)} copy(bf16[16,8,128,256]{3,2,1,0:T(8,128)(2,1)} %bitcast.42) | data formatting | bytes 16777216
  526.9 11.9 %copy.12 = bf16[32768,128]{1,0:T(8,128)(2,1)} copy(bf16[32768,128]{0,1:T(8,128)(2,1)} %bitcast.45) | data formatting | bytes 16777216 | tf_op jit(solution)/shard_map/dot_general | solution.py:60
  538.8 9.0 %fusion = bf16[1,76,128,256]{3,1,2,0:T(8,128)(2,1)} fusion(pred[128,256]{1,0:T(8,128)(4,1)S(1)} %get-tuple-element.25, bf16[128,256,128]{2,1,0:T(8,128)(2,1)} %bitcast.40, f32[128]{0:T(128)S(1)} %get-tuple-element.36, f32[128]{0:T(128)S(1)} %get-tuple-element.35), kind=kOutput, calls=%fused_computation.7 | convolution fusion | flops 642563584 | bytes 13403136 | tf_op jit(solution)/shard_map/dot_general | solution.py:60
  547.8 5.5 fusion.1
  553.3 9.0 %pad_maximum_fusion = bf16[2,76,128,256]{3,1,2,0:T(8,128)(2,1)} fusion(bf16[1,76,128,256]{3,1,2,0:T(8,128)(2,1)} %fusion.1, bf16[1,76,128,256]{3,1,2,0:T(8,128)(2,1)} %fusion), kind=kLoop, calls=%fused_computation.2 | loop fusion | flops 4980736 | bytes 19922944 | tf_op jit(solution)/shard_map/stack | solution.py:89
  562.3 11.6 %copy.13 = bf16[2,76,128,256]{3,2,1,0:T(8,128)(2,1)} copy(bf16[2,76,128,256]{3,1,2,0:T(8,128)(2,1)} %pad_maximum_fusion) | data formatting | bytes 19922944 | tf_op jit(solution)/shard_map/stack | solution.py:89
  (165 shorter events, 54.7 us)
Async XLA Ops:
  6.5 215.6 %all-gather.2.cloned.1.call-start = ((), (), s32[]{:S(2)}) async-start(), calls=%async_computation | async-start | bytes 8912896 | tf_op jit(solution)/shard_map/all_gather | solution.py:75
  97.0 372.9 %all-reduce.4.cloned.1.call-start = ((), (), s32[]{:S(2)}) async-start(), calls=%async_computation.1 | async-start | bytes 16777216 | tf_op jit(solution)/shard_map/psum | solution.py:13
  538.8 9.0 %copy-start = (bf16[32768,128]{1,0:T(8,128)(2,1)S(1)}, bf16[32768,128]{1,0:T(8,128)(2,1)}, u32[]{:S(2)}) copy-start(bf16[32768,128]{1,0:T(8,128)(2,1)} %copy.12) | copy-start | bytes 25165828
Sparse Core Ops, SparseCore 0:
  97.1 124.9 all-gather.1
  233.7 236.2 all-reduce.3
where the time goes:
time: 584 us; the launch traced here: 581 us
  waiting for transfers between devices  359 us (61%)
  local copies, waits for them, and re-layouts  148 us (25%)
  matrix products  35.6 us (6%)
  other arithmetic  23.6 us (4%)
  between operations  14.7 us (3%)
    psum x1, waiting for transfers between devices, broadcast(): return lax.psum(kept, axis)  236 us
    all_gather x1, waiting for transfers between devices, local(): receiver_block = lax.all_gather(local_spectrum, 'src', axis=1, tiled=True)  122 us
    gather x192, local copies, waits for them, and re-layouts  85.4 us
    unnamed x4, local copies, waits for them, and re-layouts  24.9 us
    dot_general x2, local copies, waits for them, and re-layouts, correlate(): jnp.dot(lag_table.T, cross_spectrum.reshape(bin_count, src_count * receiv...  23.2 us
    dot_general x2, matrix products, correlate(): jnp.einsum('mdt,mpt->mdp', source_block, receiver_block, preferred_elemen...  20.8 us
    dot_general x2, matrix products, correlate(): jnp.dot(lag_table.T, cross_spectrum.reshape(bin_count, src_count * receiv...  14.5 us
  transfers between devices with their start and end apart: 2, of which 2 were waited for; matrix products, arithmetic and copies ran while one was open for 0% of the time, Pallas kernels for 0%

commit v1 on v0

v1 whole, which is shorter than its diff:
```python
import functools

import jax
import jax.numpy as jnp
import numpy as np
from jax import lax
from jax.experimental import pallas as pl
from jax.experimental.pallas import tpu as pltpu
from jax.sharding import PartitionSpec as P

L = 256
SB = 128
LAGS = 76
LAGP = 80
BINS = L // 2
LANES = 128
SPAN = L + LANES
STRIDE = 128
GROUP = 16


def tables(win_count):
    sample_axis = np.arange(L, dtype=np.float32)
    bin_axis = np.arange(BINS, dtype=np.float32)
    two_pi = np.float32(2.0 * np.pi)
    phases = two_pi * sample_axis[:, None] * bin_axis[None, :] / np.float32(L)
    taper = np.float32(0.5) - np.float32(0.5) * np.cos(two_pi * sample_axis / np.float32(L))
    dft = np.concatenate([taper[:, None] * np.cos(phases), -taper[:, None] * np.sin(phases)], axis=1)
    dft = dft.astype(jnp.bfloat16).astype(np.float32)
    shifted = np.zeros((L, SPAN), np.float32)
    shifted[:, :L] = dft.T
    lag_axis = np.arange(LAGS, dtype=np.float32)
    weights = np.where(bin_axis == 0, 1.0, 2.0).astype(np.float32)
    lag = (
        weights[:, None]
        * np.cos(two_pi * bin_axis[:, None] * lag_axis[None, :] / np.float32(L))
        * np.float32(2.0 / (win_count * L))
    )
    lag_t = np.zeros((LAGP, BINS), np.float32)
    lag_t[:LAGS] = lag.T
    return shifted, lag_t.astype(jnp.bfloat16)


def compute_kernel(off_ref, chan_ref, dft_ref, lag_ref, rcv_ref, src_ref, out_ref,
                   spec_rcv, spec_src, wide, lagged):
    turn, group = pl.program_id(0), pl.program_id(1)
    win_count = off_ref.shape[0]
    taps = 2 * win_count
    last = rcv_ref.shape[1] // LANES - SPAN // LANES

    def spectra(records_ref, store):
        @pl.loop(0, win_count)
        def _(w):
            first = off_ref[w]
            base = jnp.minimum(first // LANES, last)
            table = pltpu.roll(dft_ref[...], first - base * LANES, 1).astype(jnp.bfloat16)
            samples = records_ref[:, pl.ds(pl.multiple_of(base * LANES, LANES), SPAN)]
            value = lax.dot_general(table, samples, (((1,), (1,)), ((), ())),
                                    preferred_element_type=jnp.float32)
            for half in range(2):
                for part in range(2):
                    wide[half, pl.ds(part * win_count + w, BINS, stride=STRIDE), :] = (
                        value[part * BINS:(part + 1) * BINS, half * LANES:(half + 1) * LANES])

        @pl.loop(0, BINS)
        def _(f):
            for half in range(2):
                rows = wide[half, pl.ds(pl.multiple_of(f * STRIDE, 8), taps), :]
                store(f, half, rows.astype(jnp.bfloat16))

    @pl.when((turn == 0) & (group == 0))
    def _():
        def to_rcv(f, half, rows):
            spec_rcv[f, :, half * LANES:(half + 1) * LANES] = rows

        def to_src(f, half, rows):
            spec_src[half, f] = rows

        spectra(rcv_ref, to_rcv)
        spectra(src_ref, to_src)

    @pl.when(group == 0)
    def _():
        @pl.loop(0, BINS, unroll=2)
        def _(f):
            value = lax.dot_general(spec_src[turn, f], spec_rcv[f], (((0,), (0,)), ((), ())),
                                    preferred_element_type=jnp.float32)
            for half in range(2):
                wide[half, pl.ds(f, SB, stride=STRIDE), :] = value[:, half * LANES:(half + 1) * LANES]

    for s in range(GROUP):
        begin = pl.multiple_of((group * GROUP + s) * STRIDE, 8)
        for half in range(2):
            pass
        cross = jnp.concatenate(
            [wide[half, pl.ds(begin, BINS), :].astype(jnp.bfloat16) for half in range(2)], axis=1)
        value = jnp.dot(lag_ref[...], cross, preferred_element_type=jnp.float32)
        for half in range(2):
            lagged[half, pl.ds(s, LAGP, stride=GROUP), :] = value[:, half * LANES:(half + 1) * LANES]
    src_chan = chan_ref[turn] + group * GROUP + lax.broadcasted_iota(jnp.int32, (GROUP, LANES), 0)
    for half in range(2):
        rcv_chan = chan_ref[2] + half * LANES + lax.broadcasted_iota(jnp.int32, (GROUP, LANES), 1)
        apart = src_chan != rcv_chan
        for lag in range(LAGS):
            value = lagged[half, lag * GROUP:(lag + 1) * GROUP, :]
            out_ref[0, lag, :, half * LANES:(half + 1) * LANES] = (
                jnp.where(apart, value, 0.0).astype(jnp.bfloat16))


def compute(offsets, chans, rcv, src):
    win_count = offsets.shape[0]
    turns = src.shape[0] // SB
    rcv_total = rcv.shape[0]
    dft, lag = tables(win_count)
    taps = 2 * win_count
    whole = lambda shape: pl.BlockSpec(shape, lambda t, g, *_: (0,) * len(shape), pipeline_mode=pl.Buffered(1))
    return pl.pallas_call(
        compute_kernel,
        name="correlate",
        grid_spec=pltpu.PrefetchScalarGridSpec(
            num_scalar_prefetch=2,
            grid=(turns, SB // GROUP),
            in_specs=[whole(dft.shape), whole(lag.shape), whole(rcv.shape), whole(src.shape)],
            out_specs=pl.BlockSpec((1, LAGS, GROUP, rcv_total), lambda t, g, *_: (t, 0, g, 0)),
            scratch_shapes=[
                pltpu.VMEM((BINS, taps, rcv_total), jnp.bfloat16),
                pltpu.VMEM((turns, BINS, taps, SB), jnp.bfloat16),
                pltpu.VMEM((2, BINS * STRIDE, LANES), jnp.float32),
                pltpu.VMEM((2, LAGP * GROUP, LANES), jnp.float32),
            ],
        ),
        out_shape=jax.ShapeDtypeStruct((turns, LAGS, SB, rcv_total), jnp.bfloat16),
        compiler_params=pltpu.CompilerParams(vmem_limit_bytes=56 * 1024 * 1024),
    )(offsets, chans, dft, lag, rcv, src)


def local(records, live_mask, offsets, block_ids):
    members = records.shape[0] * lax.axis_size("src")
    live_rec = records * live_mask[:, None].astype(records.dtype)
    rcv = lax.all_gather(live_rec, "src", axis=0, tiled=True)
    first = block_ids[:, 0] * SB
    group = lax.axis_index("rcv")
    pieces = []
    for turn in range(block_ids.shape[0]):
        piece = lax.dynamic_slice_in_dim(rcv, first[turn] % members, SB, 0)
        pieces.append(jnp.where(first[turn] // members == group, piece, 0).astype(piece.dtype))
    src = lax.psum(jnp.concatenate(pieces), "rcv")
    chans = jnp.concatenate([first, (group * members)[None].astype(jnp.int32)])
    return compute(offsets, chans, rcv, src)


def solution(mesh):
    in_specs = (P(("rcv", "src"), None), P(("rcv", "src")), P(), P(None, "src"))
    out_specs = P(None, None, "src", "rcv")
    return jax.shard_map(local, mesh=mesh, in_specs=in_specs, out_specs=out_specs, check_vma=False)
```

time: 584 us -> 435 us (0.74)
  local copies, waits for them, and re-layouts: 148 us -> 0.61 us
  Pallas kernels: 0 us -> 128 us
  waiting for transfers between devices: 359 us -> 277 us
  matrix products: 35.6 us -> 0 us
  other arithmetic: 23.6 us -> 9.63 us
    pallas_call x0 -> x1, Pallas kernels: none -> 128 us  [compute(): pl.pallas_call(compute_kernel, name='correlate', grid_spec=pltpu.Prefetch...]
    gather x192 -> x0, local copies, waits for them, and re-layouts: 85.4 us -> none
    all_gather x1, waiting for transfers between devices: 122 us -> 77.1 us  [local(): rcv = lax.all_gather(live_rec, 'src', axis=0, tiled=True)]
    psum x1, waiting for transfers between devices: 236 us -> 200 us  [local(): src = lax.psum(jnp.concatenate(pieces), 'rcv')]
    dot_general x5 -> x0, matrix products: 35.6 us -> none  [the longest x2 20.8 us: correlate(): jnp.einsum('mdt,mpt->mdp', source_block, receiver_block, preferred_elemen...]
    unnamed x4 -> x0, local copies, waits for them, and re-layouts: 24.9 us -> none
    dot_general x2 -> x0, local copies, waits for them, and re-layouts: 23.2 us -> none  [correlate(): jnp.dot(lag_table.T, cross_spectrum.reshape(bin_count, src_count * receiv...]
    another operation x1 -> x0, local copies, waits for them, and re-layouts: 11.6 us -> none  [local(): return jnp.stack(results)]
where the time goes in v1:
time: 435 us; the launch traced here: 433 us
  waiting for transfers between devices  277 us (64%)
  Pallas kernels  128 us (29%)
  between operations  18.4 us (4%)
  other arithmetic  9.63 us (2%)
    psum x1, waiting for transfers between devices, local(): src = lax.psum(jnp.concatenate(pieces), 'rcv')  200 us
    pallas_call x1, Pallas kernels, compute(): pl.pallas_call(compute_kernel, name='correlate', grid_spec=pltpu.Prefetch...  128 us
    all_gather x1, waiting for transfers between devices, local(): rcv = lax.all_gather(live_rec, 'src', axis=0, tiled=True)  77.1 us
  transfers between devices with their start and end apart: 2, of which 2 were waited for; matrix products, arithmetic and copies ran while one was open for 0% of the time, Pallas kernels for 0%

profile of v1, /device:TPU:1, one launch (start us, length us, event | category | flops | bytes accessed | tf_op | source)
XLA Modules:
  0.0 433.5 jit_solution(2455848563716703428)
XLA Ops:
  6.5 0.0 all-gather.2.cloned.1.call-start
  6.5 0.7 convert_element_type.7
  7.2 1.7 broadcast_multiply_fusion
  8.9 0.0 all-gather.2.cloned.1.call-update
  9.0 0.0 all-reduce.2.cloned.1.call-start
  9.0 0.7 broadcast_multiply_fusion.1
  9.7 0.6 fusion.1
  15.2 77.1 %all-gather.2.cloned.1.call-done.rcv_ref = bf16[256,8192]{1,0:T(8,128)(2,1)} async-done(((bf16[16,8192]{1,0:T(8,128)(2,1)}), bf16[256,8192]{1,0:T(8,128)(2,1)}) %all-gather.2.cloned.1.call-update) | async-done | bytes 4194320 | tf_op jit(solution)/shard_map/all_gather | solution.py:140
  92.3 3.5 dynamic-slice_select_fusion.1
  95.8 2.5 pad_maximum_fusion
  98.3 0.0 all-reduce.2.cloned.1.call-update
  98.3 0.6 pad_add_fusion.chan_ref
  98.9 200.2 %all-reduce.2.cloned.1.call-done.src_ref = bf16[256,8192]{1,0:T(8,128)(2,1)} async-done(((bf16[256,8192]{1,0:T(8,128)(2,1)}), bf16[256,8192]{1,0:T(8,128)(2,1)}) %all-reduce.2.cloned.1.call-update) | async-done | bytes 4194320 | tf_op jit(solution)/shard_map/psum | solution.py:147
  299.1 127.5 %correlate.1 = bf16[2,76,128,256]{3,2,1,0:T(8,128)(2,1)} custom-call(s32[64]{0:T(128)} %off_ref.1, s32[3]{0:T(128)} %pad_add_fusion.chan_ref, f32[256,384]{1,0:T(8,128)} %constant.50.clone.dft_ref, bf16[80,128]{1,0:T(8,128)(2,1)} %constant.51.clone.lag_ref, bf16[256,8192]{1,0:T(8,128)(2,1)} %all-gather.2.cloned.1.call-done.rcv_ref, ...), custom_call_target="tpu_custom_call" | custom-call | tf_op jit(solution)/shard_map/correlate/pallas_call | solution.py:117
Async XLA Ops:
  6.5 85.8 %all-gather.2.cloned.1.call-start = ((), (), s32[]{:S(2)}) async-start(), calls=%async_computation | async-start | bytes 4456448 | tf_op jit(solution)/shard_map/all_gather | solution.py:140
  9.0 290.1 %all-reduce.2.cloned.1.call-start = ((), (), s32[]{:S(2)}) async-start(), calls=%async_computation.1 | async-start | bytes 8388608 | tf_op jit(solution)/shard_map/psum | solution.py:147
Sparse Core Ops, SparseCore 0:
  9.1 83.1 all-gather.1
  98.4 200.6 all-reduce.1

commit v2 on v1

--- a/solution.py
+++ b/solution.py
@@ -1,5 +1,3 @@
-import functools
-
 import jax
 import jax.numpy as jnp
 import numpy as np
@@ -15,7 +13,7 @@
 BINS = L // 2
 LANES = 128
 SPAN = L + LANES
-STRIDE = 128
+STRIDE = 136
 GROUP = 16
 
 
@@ -90,8 +88,6 @@
 
     for s in range(GROUP):
         begin = pl.multiple_of((group * GROUP + s) * STRIDE, 8)
-        for half in range(2):
-            pass
         cross = jnp.concatenate(
             [wide[half, pl.ds(begin, BINS), :].astype(jnp.bfloat16) for half in range(2)], axis=1)
         value = jnp.dot(lag_ref[...], cross, preferred_element_type=jnp.float32)
@@ -134,17 +130,222 @@
     )(offsets, chans, dft, lag, rcv, src)
 
 
+NX, NY, NZ, NC = 4, 4, 8, 2
+ZL = NZ // 2
+PIECES = 2
+MESH = pl.DeviceIdType.MESH
+
+
+def gather_kernel(rec_ref, live_ref, ids_ref, rcv_ref, src_ref, *scratch):
+    columns = scratch[:PIECES]
+    picked = scratch[PIECES:2 * PIECES]
+    offered = scratch[2 * PIECES:3 * PIECES]
+    chosen = scratch[3 * PIECES:4 * PIECES]
+    merged = scratch[4 * PIECES:5 * PIECES]
+    (id_buf, id_smem, z_send, z_recv, c_send, c_recv, x_send, x_recv, y_send, y_recv,
+     g_send, g_recv, e_send, e_recv, r_send, r_recv, f_send, f_recv, i_send, i_recv,
+     local_sem) = scratch[5 * PIECES:]
+    shard, total = rec_ref.shape
+    width = total // PIECES
+    part = width // NX
+
+    src, rcv = lax.axis_index("src"), lax.axis_index("rcv")
+    y, zl = src % NY, src // NY
+    core, x, zh = rcv % NC, (rcv // NC) % NX, rcv // (NC * NX)
+    z = zh * ZL + zl
+
+    def device(x_to=x, y_to=y, z_to=z, core_to=core):
+        return {"src": (z_to % ZL) * NY + y_to,
+                "rcv": ((z_to // ZL) * NX + x_to) * NC + core_to}
+
+    def send(src_ref, dst_ref, send_sem, recv_sem, to):
+        copy = pltpu.make_async_remote_copy(
+            src_ref=src_ref, dst_ref=dst_ref, send_sem=send_sem, recv_sem=recv_sem,
+            device_id=to, device_id_type=MESH)
+        copy.start()
+        return copy
+
+    z_up, z_down = (z + 1) % NZ, (z + NZ - 1) % NZ
+    sibling = device(core_to=1 - core)
+
+    barrier = pltpu.get_barrier_semaphore()
+    peers = [device(z_to=z_up), device(z_to=z_down), sibling]
+    peers += [device(x_to=(x + d) % NX) for d in range(1, NX)]
+    peers += [device(y_to=(y + d) % NY) for d in range(1, NY)]
+    for peer in peers:
+        pl.semaphore_signal(barrier, inc=1, device_id=peer, device_id_type=MESH)
+
+    live = live_ref[:, :1]
+    for t in range(PIECES):
+        columns[t][core, z] = rec_ref[:, t * width:(t + 1) * width] * live
+    id_buf[y] = ids_ref[...]
+    pl.semaphore_wait(barrier, len(peers))
+
+    started = []
+    ids = [send(ids_ref, id_buf.at[y], i_send.at[d - 1], i_recv.at[d - 1],
+                device(y_to=(y + d) % NY)) for d in range(1, NY)]
+
+    def z_hop(t, way, hop):
+        slot = (z - (hop - 1) + NZ) % NZ if way == 0 else (z + (hop - 1)) % NZ
+        return send(columns[t].at[core, slot], columns[t].at[core, slot],
+                    z_send.at[t, way, hop - 1], z_recv.at[t, way, hop - 1],
+                    device(z_to=z_up if way == 0 else z_down))
+
+    def to_sibling(t, slot, index):
+        return send(columns[t].at[core, slot], columns[t].at[core, slot],
+                    c_send.at[t, index], c_recv.at[t, index], sibling)
+
+    hops = [(4, 3) if t % 2 == 0 else (3, 4) for t in range(PIECES)]
+    flying = {}
+    shared = [[] for _ in range(PIECES)]
+    for t in range(PIECES):
+        for way in range(2):
+            flying[t, way] = z_hop(t, way, 1)
+        shared[t].append(to_sibling(t, z, 0))
+    for hop in range(1, NZ // 2 + 1):
+        for t in range(PIECES):
+            for way in range(2):
+                if hop > hops[t][way]:
+                    continue
+                flying[t, way].wait_recv()
+                started.append(flying[t, way])
+                if hop < hops[t][way]:
+                    flying[t, way] = z_hop(t, way, hop + 1)
+                slot = (z - hop + NZ) % NZ if way == 0 else (z + hop) % NZ
+                shared[t].append(to_sibling(t, slot, hop + way * hops[t][0]))
+
+    for copy in ids:
+        copy.wait()
+    to_smem = pltpu.make_async_copy(id_buf, id_smem, local_sem.at[0])
+    to_smem.start()
+    to_smem.wait()
+
+    def columns_span(t):
+        return pl.ds(t * width, width)
+
+    ring, mine, exchanged, spread, gathered, twins = [], [], [], [], [], []
+    for t in range(PIECES):
+        own = columns[t].at[core, pl.ds(zh * ZL, ZL)]
+        target = rcv_ref.at[:, y, :, columns_span(t)]
+        ring.append([send(own, target, r_send.at[t, way], r_recv.at[t, way],
+                          device(y_to=(y + (1 if way == 0 else NY - 1)) % NY)) for way in range(2)])
+        copy = pltpu.make_async_copy(own, target, local_sem.at[1 + t])
+        copy.start()
+        mine.append(copy)
+
+        for copy in shared[t]:
+            copy.wait_recv()
+        started += shared[t]
+        for y_of in range(NY):
+            block = id_smem[y_of, core, 0]
+            group = block // 2
+            slot = (group // (NC * NX)) * ZL + (block % 2) * 2
+            for p in range(2):
+                for q in range(NX):
+                    picked[t][q, y_of, p] = columns[t][group % NC, slot + p, :, q * part:(q + 1) * part]
+        exchanged.append([send(picked[t].at[(x + d) % NX], offered[t].at[x], x_send.at[t, d - 1],
+                               x_recv.at[t, d - 1], device(x_to=(x + d) % NX)) for d in range(1, NX)])
+        offered[t][x] = picked[t][x]
+
+    forward = []
+    for t in range(PIECES):
+        for copy in exchanged[t]:
+            copy.wait_recv()
+        started += exchanged[t]
+        for y_of in range(NY):
+            group = id_smem[y_of, core, 0] // 2
+            chosen[t][y_of] = offered[t][(group // NC) % NX, y_of]
+        spread.append([send(chosen[t].at[(y + d) % NY], merged[t].at[:, y], y_send.at[t, d - 1],
+                            y_recv.at[t, d - 1], device(y_to=(y + d) % NY)) for d in range(1, NY)])
+        for p in range(2):
+            merged[t][p, y] = chosen[t][y, p]
+        way = t % 2
+        ring[t][way].wait_recv()
+        from_y = (y + NY - 1) % NY if way == 0 else (y + 1) % NY
+        to_y = (y + 1) % NY if way == 0 else (y + NY - 1) % NY
+        forward.append(send(rcv_ref.at[:, from_y, :, columns_span(t)],
+                            rcv_ref.at[:, from_y, :, columns_span(t)],
+                            f_send.at[t], f_recv.at[t], device(y_to=to_y)))
+
+    for t in range(PIECES):
+        for copy in spread[t]:
+            copy.wait_recv()
+        started += spread[t]
+        place = src_ref.at[core, :, :, :, pl.ds(t * width + x * part, part)]
+        gathered.append([send(merged[t], place, g_send.at[t, d - 1], g_recv.at[t, d - 1],
+                              device(x_to=(x + d) % NX)) for d in range(1, NX)])
+        copy = pltpu.make_async_copy(merged[t], place, local_sem.at[1 + PIECES + t])
+        copy.start()
+        mine.append(copy)
+
+    for t in range(PIECES):
+        for copy in gathered[t]:
+            copy.wait_recv()
+        started += gathered[t]
+        mine[PIECES + t].wait()
+        whole = src_ref.at[core, :, :, :, columns_span(t)]
+        twins.append(send(whole, whole, e_send.at[t], e_recv.at[t], sibling))
+
+    for t in range(PIECES):
+        mine[t].wait()
+        ring[t][1 - t % 2].wait_recv()
+        forward[t].wait_recv()
+        twins[t].wait_recv()
+        for copy in ring[t] + [forward[t], twins[t]]:
+            copy.wait_send()
+    for copy in started:
+        copy.wait_send()
+
+
+def gather(records, live_mask, block_ids):
+    shard, total = records.shape
+    width = total // PIECES
+    turns = block_ids.shape[0]
+    live = jnp.broadcast_to(live_mask[:, None].astype(records.dtype), (shard, LANES))
+    ids = jnp.zeros((8, LANES), jnp.int32).at[:turns].set(block_ids)
+    dma = pltpu.SemaphoreType.DMA
+    vmem = pl.BlockSpec(memory_space=pltpu.VMEM)
+    part = width // NX
+    rcv, src = pl.pallas_call(
+        gather_kernel,
+        name="gather",
+        in_specs=[vmem] * 3,
+        out_specs=[vmem] * 2,
+        out_shape=[
+            jax.ShapeDtypeStruct((ZL, NY, shard, total), records.dtype),
+            jax.ShapeDtypeStruct((turns, 2, NY, shard, total), records.dtype),
+        ],
+        scratch_shapes=(
+            [pltpu.VMEM((NC, NZ, shard, width), records.dtype)] * PIECES
+            + [pltpu.VMEM((NX, NY, 2, shard, part), records.dtype)] * (2 * PIECES)
+            + [pltpu.VMEM((NY, 2, shard, part), records.dtype)] * PIECES
+            + [pltpu.VMEM((2, NY, shard, part), records.dtype)] * PIECES
+            + [
+                pltpu.VMEM((NY, 8, LANES), jnp.int32),
+                pltpu.SMEM((NY, 8, LANES), jnp.int32),
+                dma((PIECES, 2, 4)), dma((PIECES, 2, 4)),
+                dma((PIECES, NZ)), dma((PIECES, NZ)),
+                dma((PIECES, 3)), dma((PIECES, 3)),
+                dma((PIECES, 3)), dma((PIECES, 3)),
+                dma((PIECES, 3)), dma((PIECES, 3)),
+                dma((PIECES,)), dma((PIECES,)),
+                dma((PIECES, 2)), dma((PIECES, 2)),
+                dma((PIECES,)), dma((PIECES,)),
+                dma((3,)), dma((3,)),
+                dma((1 + 2 * PIECES,)),
+            ]
+        ),
+        compiler_params=pltpu.CompilerParams(
+            collective_id=0, has_side_effects=True, vmem_limit_bytes=40 * 1024 * 1024),
+    )(records, live, ids)
+    return rcv.reshape(-1, total), src.reshape(-1, total)
+
+
 def local(records, live_mask, offsets, block_ids):
     members = records.shape[0] * lax.axis_size("src")
-    live_rec = records * live_mask[:, None].astype(records.dtype)
-    rcv = lax.all_gather(live_rec, "src", axis=0, tiled=True)
+    rcv, src = gather(records, live_mask, block_ids)
     first = block_ids[:, 0] * SB
     group = lax.axis_index("rcv")
-    pieces = []
-    for turn in range(block_ids.shape[0]):
-        piece = lax.dynamic_slice_in_dim(rcv, first[turn] % members, SB, 0)
-        pieces.append(jnp.where(first[turn] // members == group, piece, 0).astype(piece.dtype))
-    src = lax.psum(jnp.concatenate(pieces), "rcv")
     chans = jnp.concatenate([first, (group * members)[None].astype(jnp.int32)])
     return compute(offsets, chans, rcv, src)
 

time: 435 us -> 181 us (0.42)
  waiting for transfers between devices: 277 us -> 0 us
  Pallas kernels: 128 us -> 173 us
  between operations: 18.4 us -> 0.02 us
  other arithmetic: 9.63 us -> 1.87 us
  local copies, waits for them, and re-layouts: 0.61 us -> 5.65 us
    psum x1 -> x0, waiting for transfers between devices: 200 us -> none  [local(): src = lax.psum(jnp.concatenate(pieces), 'rcv')]
    pallas_call x0 -> x1, Pallas kernels: none -> 86.7 us  [gather(): pl.pallas_call(gather_kernel, name='gather', in_specs=[vmem] * 3, out_spe...]
    all_gather x1 -> x0, waiting for transfers between devices: 77.1 us -> none  [local(): rcv = lax.all_gather(live_rec, 'src', axis=0, tiled=True)]
    pallas_call x1, Pallas kernels: 128 us -> 86.4 us  [compute(): pl.pallas_call(compute_kernel, name='correlate', grid_spec=pltpu.Prefetch...]
    unnamed x0 -> x6, local copies, waits for them, and re-layouts: none -> 4.85 us
  transfers between devices with their start and end apart: 2 -> 0, of which waited for: 2 -> 0; matrix products, arithmetic and copies ran while one was open for 0% -> 0% of each run, Pallas kernels for 0% -> 0%
where the time goes in v2:
time: 181 us
  Pallas kernels  173 us (96%)
  local copies, waits for them, and re-layouts  5.65 us (3%)
  other arithmetic  1.87 us (1%)
    pallas_call x1, Pallas kernels, gather(): pl.pallas_call(gather_kernel, name='gather', in_specs=[vmem] * 3, out_spe...  86.7 us
    pallas_call x1, Pallas kernels, compute(): pl.pallas_call(compute_kernel, name='correlate', grid_spec=pltpu.Prefetch...  86.4 us
    unnamed x6, local copies, waits for them, and re-layouts  4.85 us

profile of v2, /device:TPU:1, one launch (start us, length us, event | category | flops | bytes accessed | tf_op | source)
XLA Modules:
  0.0 180.6 jit_solution(12311464987113099839)
XLA Ops:
  0.0 0.7 convert_element_type.4
  0.7 0.7 scatter.7
  1.3 0.7 broadcast_multiply_fusion
  2.0 0.6 pad_add_fusion.chan_ref
  2.5 0.1 scatter.8.ids_ref
  2.6 0.1 broadcast_in_dim.5.live_ref
  2.7 0.0 copy-start.2
  2.7 0.9 copy-done.2
  3.6 86.7 %gather.1 = (bf16[4,4,16,8192]{3,2,1,0:T(8,128)(2,1)S(1)}, bf16[2,2,4,16,8192]{4,3,2,1,0:T(8,128)(2,1)S(1)}) custom-call(bf16[16,8192]{1,0:T(8,128)(2,1)S(1)} %copy-done.2, bf16[16,128]{1,0:T(8,128)(2,1)S(1)} %broadcast_in_dim.5.live_ref, s32[8,128]{1,0:T(8,128)S(1)} %scatter.8.ids_ref), custom_call_target="tpu_custom_call" | custom-call | tf_op jit(solution)/shard_map/gather/pallas_call | solution.py:309
  90.3 0.0 copy-start
  90.4 1.9 %copy-done = bf16[4,4,16,8192]{3,2,1,0:T(8,128)(2,1)} copy-done((bf16[4,4,16,8192]{3,2,1,0:T(8,128)(2,1)}, bf16[4,4,16,8192]{3,2,1,0:T(8,128)(2,1)S(1)}, u32[]{:S(2)}) %copy-start) | copy-done | bytes 4194328
  92.3 0.0 copy-start.1
  92.3 2.0 %copy-done.1 = bf16[2,2,4,16,8192]{4,3,2,1,0:T(8,128)(2,1)} copy-done((bf16[2,2,4,16,8192]{4,3,2,1,0:T(8,128)(2,1)}, bf16[2,2,4,16,8192]{4,3,2,1,0:T(8,128)(2,1)S(1)}, u32[]{:S(2)}) %copy-start.1) | copy-done | bytes 4194328
  94.3 86.4 %correlate.1 = bf16[2,76,128,256]{3,2,1,0:T(8,128)(2,1)} custom-call(s32[64]{0:T(128)} %off_ref.1, s32[3]{0:T(128)} %pad_add_fusion.chan_ref, f32[256,384]{1,0:T(8,128)} %constant.40.clone.dft_ref, bf16[80,128]{1,0:T(8,128)(2,1)} %constant.41.clone.lag_ref, bf16[256,8192]{1,0:T(8,128)(2,1)} %bitcast.5, bf16[256,8192]{1,0:T(8,128)(2,1)} %bitcast.6), custom_call_target="tpu_custom_call" | custom-call | tf_op jit(solution)/shard_map/correlate/pallas_call | solution.py:113
Async XLA Ops:
  2.7 1.0 copy-start.2
  90.3 1.9 %copy-start = (bf16[4,4,16,8192]{3,2,1,0:T(8,128)(2,1)}, bf16[4,4,16,8192]{3,2,1,0:T(8,128)(2,1)S(1)}, u32[]{:S(2)}) copy-start(bf16[4,4,16,8192]{3,2,1,0:T(8,128)(2,1)S(1)} %get-tuple-element.19) | copy-start | bytes 12582916
  92.3 2.0 %copy-start.1 = (bf16[2,2,4,16,8192]{4,3,2,1,0:T(8,128)(2,1)}, bf16[2,2,4,16,8192]{4,3,2,1,0:T(8,128)(2,1)S(1)}, u32[]{:S(2)}) copy-start(bf16[2,2,4,16,8192]{4,3,2,1,0:T(8,128)(2,1)S(1)} %get-tuple-element.20) | copy-start | bytes 12582916

commit v3 on v1

--- a/solution.py
+++ b/solution.py
@@ -1,5 +1,3 @@
-import functools
-
 import jax
 import jax.numpy as jnp
 import numpy as np
@@ -15,8 +13,9 @@
 BINS = L // 2
 LANES = 128
 SPAN = L + LANES
-STRIDE = 128
-GROUP = 16
+STRIDE = 132
+GROUP = 32
+ROWS = 36
 
 
 def tables(win_count):
@@ -49,7 +48,7 @@
     last = rcv_ref.shape[1] // LANES - SPAN // LANES
 
     def spectra(records_ref, store):
-        @pl.loop(0, win_count)
+        @pl.loop(0, win_count, unroll=8)
         def _(w):
             first = off_ref[w]
             base = jnp.minimum(first // LANES, last)
@@ -62,10 +61,10 @@
                     wide[half, pl.ds(part * win_count + w, BINS, stride=STRIDE), :] = (
                         value[part * BINS:(part + 1) * BINS, half * LANES:(half + 1) * LANES])
 
-        @pl.loop(0, BINS)
+        @pl.loop(0, BINS, unroll=8)
         def _(f):
             for half in range(2):
-                rows = wide[half, pl.ds(pl.multiple_of(f * STRIDE, 8), taps), :]
+                rows = wide[half, pl.ds(pl.multiple_of(f * STRIDE, 4), taps), :]
                 store(f, half, rows.astype(jnp.bfloat16))
 
     @pl.when((turn == 0) & (group == 0))
@@ -81,7 +80,7 @@
 
     @pl.when(group == 0)
     def _():
-        @pl.loop(0, BINS, unroll=2)
+        @pl.loop(0, BINS, unroll=8)
         def _(f):
             value = lax.dot_general(spec_src[turn, f], spec_rcv[f], (((0,), (0,)), ((), ())),
                                     preferred_element_type=jnp.float32)
@@ -89,20 +88,18 @@
                 wide[half, pl.ds(f, SB, stride=STRIDE), :] = value[:, half * LANES:(half + 1) * LANES]
 
     for s in range(GROUP):
-        begin = pl.multiple_of((group * GROUP + s) * STRIDE, 8)
-        for half in range(2):
-            pass
+        begin = pl.multiple_of((group * GROUP + s) * STRIDE, 4)
         cross = jnp.concatenate(
             [wide[half, pl.ds(begin, BINS), :].astype(jnp.bfloat16) for half in range(2)], axis=1)
         value = jnp.dot(lag_ref[...], cross, preferred_element_type=jnp.float32)
         for half in range(2):
-            lagged[half, pl.ds(s, LAGP, stride=GROUP), :] = value[:, half * LANES:(half + 1) * LANES]
+            lagged[half, pl.ds(s, LAGP, stride=ROWS), :] = value[:, half * LANES:(half + 1) * LANES]
     src_chan = chan_ref[turn] + group * GROUP + lax.broadcasted_iota(jnp.int32, (GROUP, LANES), 0)
     for half in range(2):
         rcv_chan = chan_ref[2] + half * LANES + lax.broadcasted_iota(jnp.int32, (GROUP, LANES), 1)
         apart = src_chan != rcv_chan
         for lag in range(LAGS):
-            value = lagged[half, lag * GROUP:(lag + 1) * GROUP, :]
+            value = lagged[half, lag * ROWS:lag * ROWS + GROUP, :]
             out_ref[0, lag, :, half * LANES:(half + 1) * LANES] = (
                 jnp.where(apart, value, 0.0).astype(jnp.bfloat16))
 
@@ -126,7 +123,7 @@
                 pltpu.VMEM((BINS, taps, rcv_total), jnp.bfloat16),
                 pltpu.VMEM((turns, BINS, taps, SB), jnp.bfloat16),
                 pltpu.VMEM((2, BINS * STRIDE, LANES), jnp.float32),
-                pltpu.VMEM((2, LAGP * GROUP, LANES), jnp.float32),
+                pltpu.VMEM((2, LAGP * ROWS, LANES), jnp.float32),
             ],
         ),
         out_shape=jax.ShapeDtypeStruct((turns, LAGS, SB, rcv_total), jnp.bfloat16),
@@ -134,17 +131,261 @@
     )(offsets, chans, dft, lag, rcv, src)
 
 
+NX, NY, NZ, NC = 4, 4, 8, 2
+ZL = NZ // 2
+PIECES = 4
+SKEW = 1
+MESH = pl.DeviceIdType.MESH
+
+
+def gather_kernel(rec_ref, live_ref, ids_ref, rcv_ref, src_ref, *scratch):
+    columns, first, mixed, second, landed, chosen, merged = (
+        scratch[i * PIECES:(i + 1) * PIECES] for i in range(7))
+    (id_buf, id_smem, z_send, z_recv, c_send, c_recv, x_send, x_recv, y_send, y_recv,
+     g_send, g_recv, e_send, e_recv, r_send, r_recv, i_send, i_recv,
+     local_sem) = scratch[7 * PIECES:]
+    shard, total = rec_ref.shape
+    width = total // PIECES
+    part = width // NX
+    half = part // 2
+
+    src, rcv = lax.axis_index("src"), lax.axis_index("rcv")
+    y, zl = src % NY, src // NY
+    core, x, zh = rcv % NC, (rcv // NC) % NX, rcv // (NC * NX)
+    z = zh * ZL + zl
+
+    def device(x_to=x, y_to=y, z_to=z, core_to=core):
+        return {"src": (z_to % ZL) * NY + y_to,
+                "rcv": ((z_to // ZL) * NX + x_to) * NC + core_to}
+
+    sent = []
+
+    def send(src_ref, dst_ref, send_sem, recv_sem, to):
+        copy = pltpu.make_async_remote_copy(
+            src_ref=src_ref, dst_ref=dst_ref, send_sem=send_sem, recv_sem=recv_sem,
+            device_id=to, device_id_type=MESH)
+        copy.start()
+        sent.append(copy)
+        return copy
+
+    def step(position, way, count):
+        return (position + 1) % count if way == 0 else (position + count - 1) % count
+
+    sibling = device(core_to=1 - core)
+    barrier = pltpu.get_barrier_semaphore()
+    peers = [device(z_to=step(z, way, NZ)) for way in range(2)] + [sibling]
+    peers += [device(x_to=step(x, way, NX)) for way in range(2)]
+    peers += [device(y_to=(y + d) % NY) for d in range(1, NY)]
+    for peer in peers:
+        pl.semaphore_signal(barrier, inc=1, device_id=peer, device_id_type=MESH)
+
+    live = live_ref[:, :1]
+    for t in range(PIECES):
+        columns[t][core, z] = rec_ref[:, t * width:(t + 1) * width] * live
+    id_buf[y] = ids_ref[...]
+    pl.semaphore_wait(barrier, len(peers))
+
+    ids = [send(ids_ref, id_buf.at[y], i_send.at[d - 1], i_recv.at[d - 1],
+                device(y_to=(y + d) % NY)) for d in range(1, NY)]
+
+    def ids_ready():
+        for copy in ids:
+            copy.wait_recv()
+        to_smem = pltpu.make_async_copy(id_buf, id_smem, local_sem.at[0])
+        to_smem.start()
+        to_smem.wait()
+
+    locals_started = []
+
+    def piece(t):
+        hops = (4, 3) if t % 2 == 0 else (3, 4)
+        lanes = pl.ds(t * width, width)
+        flying, shared = {}, []
+        state = {}
+
+        def hop_send(way, hop):
+            slot = (z - (hop - 1) + NZ) % NZ if way == 0 else (z + (hop - 1)) % NZ
+            flying[way] = send(columns[t].at[core, slot], columns[t].at[core, slot],
+                               z_send.at[t, way, hop - 1], z_recv.at[t, way, hop - 1],
+                               device(z_to=step(z, way, NZ)))
+
+        def share(slot, index):
+            shared.append(send(columns[t].at[core, slot], columns[t].at[core, slot],
+                               c_send.at[t, index], c_recv.at[t, index], sibling))
+
+        def begin():
+            for way in range(2):
+                hop_send(way, 1)
+            share(z, 0)
+
+        def hop_stage(hop):
+            def run():
+                for way in range(2):
+                    if hop <= hops[way]:
+                        flying[way].wait_recv()
+                        if hop < hops[way]:
+                            hop_send(way, hop + 1)
+                        share((z - hop + NZ) % NZ if way == 0 else (z + hop) % NZ, hop + way * hops[0])
+            return run
+
+        def receivers():
+            own = columns[t].at[core, pl.ds(zh * ZL, ZL)]
+            target = rcv_ref.at[:, y, :, lanes]
+            state["ring"] = [send(own, target, r_send.at[t, way], r_recv.at[t, way],
+                                  device(y_to=step(y, way, NY))) for way in range(2)]
+            copy = pltpu.make_async_copy(own, target, local_sem.at[1 + t])
+            copy.start()
+            locals_started.append(copy)
+
+        def receivers_on():
+            way = t % 2
+            state["ring"][way].wait_recv()
+            held = rcv_ref.at[:, step(y, 1 - way, NY), :, lanes]
+            state["on"] = send(held, held, r_send.at[t, 2], r_recv.at[t, 2], device(y_to=step(y, way, NY)))
+
+        def pick():
+            if t == 0:
+                ids_ready()
+            for copy in shared:
+                copy.wait_recv()
+
+            for y_of in range(NY):
+                block = id_smem[y_of, core, 0]
+                group = block // 2
+                slot = (group // (NC * NX)) * ZL + (block % 2) * 2
+                for p in range(2):
+                    def take(q, h):
+                        start = pl.multiple_of(q * part + h * half, half)
+                        return columns[t][group % NC, slot + p, :, pl.ds(start, half)]
+
+                    for h in range(2):
+                        first[t][h, y_of, p] = take((x + 2) % NX, h)
+                        landed[t][4 + h, y_of, p] = take(x, h)
+                        mixed[t][h, 0, y_of, p] = take(step(x, h, NX), h)
+                        second[t][h, 1, y_of, p] = take(step(x, h, NX), 1 - h)
+            state["x1"] = [send(first[t].at[way], mixed[t].at[way, 1], x_send.at[t, way], x_recv.at[t, way],
+                                device(x_to=step(x, way, NX))) for way in range(2)]
+
+        def blend():
+            for copy in state["x1"]:
+                copy.wait_recv()
+            state["x2"] = []
+            for way in range(2):
+                for y_of in range(NY):
+                    root = (id_smem[y_of, core, 0] // (2 * NC)) % NX
+                    other = jnp.where(root == step(x, 1 - way, NX), 1, 0)
+                    second[t][way, 0, y_of] = mixed[t][way, other, y_of]
+                state["x2"].append(send(second[t].at[way], landed[t].at[pl.ds(2 * way, 2)],
+                                        x_send.at[t, 2 + way], x_recv.at[t, 2 + way],
+                                        device(x_to=step(x, way, NX))))
+
+        def choose():
+            for copy in state["x2"]:
+                copy.wait_recv()
+            for y_of in range(NY):
+                root = (id_smem[y_of, core, 0] // (2 * NC)) % NX
+                away = (root - x + NX) % NX
+                low = jnp.where(away == 0, 4, jnp.where(away == 1, 3, 0))
+                high = jnp.where(away == 0, 5, jnp.where(away == 3, 1, 2))
+                chosen[t][y_of, :, :, :half] = landed[t][low, y_of]
+                chosen[t][y_of, :, :, half:] = landed[t][high, y_of]
+            state["y"] = [send(chosen[t].at[(y + d) % NY], merged[t].at[:, y], y_send.at[t, d - 1],
+                               y_recv.at[t, d - 1], device(y_to=(y + d) % NY)) for d in range(1, NY)]
+            for p in range(2):
+                merged[t][p, y] = chosen[t][y, p]
+
+        def spread():
+            for copy in state["y"]:
+                copy.wait_recv()
+            place = src_ref.at[core, :, :, :, pl.ds(t * width + x * part, part)]
+            state["g1"] = [send(merged[t], place, g_send.at[t, way], g_recv.at[t, way],
+                                device(x_to=step(x, way, NX))) for way in range(2)]
+            copy = pltpu.make_async_copy(merged[t], place, local_sem.at[1 + PIECES + t])
+            copy.start()
+            state["own"] = copy
+
+        def spread_on():
+            state["g2"] = []
+            for way in range(2):
+                state["g1"][way].wait_recv()
+                start = t * width + step(x, 1 - way, NX) * part + way * half
+                held = src_ref.at[core, :, :, :, pl.ds(pl.multiple_of(start, half), half)]
+                state["g2"].append(send(held, held, g_send.at[t, 2 + way], g_recv.at[t, 2 + way],
+                                        device(x_to=step(x, way, NX))))
+
+        def twin():
+            for copy in state["g2"]:
+                copy.wait_recv()
+            state["own"].wait()
+            whole = src_ref.at[core, :, :, :, lanes]
+            state["twin"] = send(whole, whole, e_send.at[t], e_recv.at[t], sibling)
+
+        def finish():
+            state["ring"][1 - t % 2].wait_recv()
+            state["on"].wait_recv()
+            state["twin"].wait_recv()
+
+        return [begin] + [hop_stage(hop) for hop in range(1, NZ // 2 + 1)] + [
+            pick, receivers, blend, choose, receivers_on, spread, spread_on, twin, finish]
+
+    pieces = [piece(t) for t in range(PIECES)]
+    for slot in range(len(pieces[0]) + SKEW * (PIECES - 1)):
+        for t in range(PIECES):
+            if 0 <= slot - SKEW * t < len(pieces[t]):
+                pieces[t][slot - SKEW * t]()
+    for copy in locals_started:
+        copy.wait()
+    for copy in sent:
+        copy.wait_send()
+
+
+def gather(records, live_mask, block_ids):
+    shard, total = records.shape
+    width = total // PIECES
+    part = width // NX
+    half = part // 2
+    turns = block_ids.shape[0]
+    live = jnp.broadcast_to(live_mask[:, None].astype(records.dtype), (shard, LANES))
+    ids = jnp.zeros((8, LANES), jnp.int32).at[:turns].set(block_ids)
+    dma = pltpu.SemaphoreType.DMA
+    vmem = pl.BlockSpec(memory_space=pltpu.VMEM)
+    buffers = [
+        (NC, NZ, shard, width),
+        (2, NY, 2, shard, half),
+        (2, 2, NY, 2, shard, half),
+        (2, 2, NY, 2, shard, half),
+        (6, NY, 2, shard, half),
+        (NY, 2, shard, part),
+        (2, NY, shard, part),
+    ]
+    counts = [(PIECES, 2, 4), (PIECES, NZ), (PIECES, 4), (PIECES, 3), (PIECES, 4), (PIECES,),
+              (PIECES, 3), (NY - 1,)]
+    rcv, src = pl.pallas_call(
+        gather_kernel,
+        name="gather",
+        in_specs=[vmem] * 3,
+        out_specs=[vmem] * 2,
+        out_shape=[
+            jax.ShapeDtypeStruct((ZL, NY, shard, total), records.dtype),
+            jax.ShapeDtypeStruct((turns, 2, NY, shard, total), records.dtype),
+        ],
+        scratch_shapes=(
+            [pltpu.VMEM(shape, records.dtype) for shape in buffers for _ in range(PIECES)]
+            + [pltpu.VMEM((NY, 8, LANES), jnp.int32), pltpu.SMEM((NY, 8, LANES), jnp.int32)]
+            + [dma(shape) for shape in counts for _ in range(2)]
+            + [dma((1 + 2 * PIECES,))]
+        ),
+        compiler_params=pltpu.CompilerParams(
+            collective_id=0, has_side_effects=True, vmem_limit_bytes=40 * 1024 * 1024),
+    )(records, live, ids)
+    return rcv.reshape(-1, total), src.reshape(-1, total)
+
+
 def local(records, live_mask, offsets, block_ids):
     members = records.shape[0] * lax.axis_size("src")
-    live_rec = records * live_mask[:, None].astype(records.dtype)
-    rcv = lax.all_gather(live_rec, "src", axis=0, tiled=True)
+    rcv, src = gather(records, live_mask, block_ids)
     first = block_ids[:, 0] * SB
     group = lax.axis_index("rcv")
-    pieces = []
-    for turn in range(block_ids.shape[0]):
-        piece = lax.dynamic_slice_in_dim(rcv, first[turn] % members, SB, 0)
-        pieces.append(jnp.where(first[turn] // members == group, piece, 0).astype(piece.dtype))
-    src = lax.psum(jnp.concatenate(pieces), "rcv")
     chans = jnp.concatenate([first, (group * members)[None].astype(jnp.int32)])
     return compute(offsets, chans, rcv, src)
 

time: 435 us -> 133 us (0.31)
  waiting for transfers between devices: 277 us -> 0 us
  between operations: 18.4 us -> 0.02 us
  other arithmetic: 9.63 us -> 1.87 us
  local copies, waits for them, and re-layouts: 0.61 us -> 5.65 us
    psum x1 -> x0, waiting for transfers between devices: 200 us -> none  [local(): src = lax.psum(jnp.concatenate(pieces), 'rcv')]
    pallas_call x1, Pallas kernels: 128 us -> 40.5 us  [compute(): pl.pallas_call(compute_kernel, name='correlate', grid_spec=pltpu.Prefetch...]
    pallas_call x0 -> x1, Pallas kernels: none -> 84.9 us  [gather(): pl.pallas_call(gather_kernel, name='gather', in_specs=[vmem] * 3, out_spe...]
    all_gather x1 -> x0, waiting for transfers between devices: 77.1 us -> none  [local(): rcv = lax.all_gather(live_rec, 'src', axis=0, tiled=True)]
    unnamed x0 -> x6, local copies, waits for them, and re-layouts: none -> 4.85 us
  transfers between devices with their start and end apart: 2 -> 0, of which waited for: 2 -> 0; matrix products, arithmetic and copies ran while one was open for 0% -> 0% of each run, Pallas kernels for 0% -> 0%
where the time goes in v3:
time: 133 us
  Pallas kernels  125 us (94%)
  local copies, waits for them, and re-layouts  5.65 us (4%)
  other arithmetic  1.87 us (1%)
    pallas_call x1, Pallas kernels, gather(): pl.pallas_call(gather_kernel, name='gather', in_specs=[vmem] * 3, out_spe...  84.9 us
    pallas_call x1, Pallas kernels, compute(): pl.pallas_call(compute_kernel, name='correlate', grid_spec=pltpu.Prefetch...  40.5 us
    unnamed x6, local copies, waits for them, and re-layouts  4.85 us

profile of v3, /device:TPU:1, one launch (start us, length us, event | category | flops | bytes accessed | tf_op | source)
XLA Modules:
  0.0 132.9 jit_solution(11504638714227593320)
XLA Ops:
  0.0 0.7 convert_element_type.4
  0.7 0.7 scatter.7
  1.3 0.7 broadcast_multiply_fusion
  2.0 0.6 pad_add_fusion.chan_ref
  2.5 0.1 scatter.8.ids_ref
  2.6 0.1 broadcast_in_dim.5.live_ref
  2.7 0.0 copy-start.2
  2.7 0.9 copy-done.2
  3.6 84.9 %gather.1 = (bf16[4,4,16,8192]{3,2,1,0:T(8,128)(2,1)S(1)}, bf16[2,2,4,16,8192]{4,3,2,1,0:T(8,128)(2,1)S(1)}) custom-call(bf16[16,8192]{1,0:T(8,128)(2,1)S(1)} %copy-done.2, bf16[16,128]{1,0:T(8,128)(2,1)S(1)} %broadcast_in_dim.5.live_ref, s32[8,128]{1,0:T(8,128)S(1)} %scatter.8.ids_ref), custom_call_target="tpu_custom_call" | custom-call | tf_op jit(solution)/shard_map/gather/pallas_call | solution.py:363
  88.5 0.0 copy-start
  88.5 1.9 %copy-done = bf16[4,4,16,8192]{3,2,1,0:T(8,128)(2,1)} copy-done((bf16[4,4,16,8192]{3,2,1,0:T(8,128)(2,1)}, bf16[4,4,16,8192]{3,2,1,0:T(8,128)(2,1)S(1)}, u32[]{:S(2)}) %copy-start) | copy-done | bytes 4194328
  90.4 0.0 copy-start.1
  90.4 2.0 %copy-done.1 = bf16[2,2,4,16,8192]{4,3,2,1,0:T(8,128)(2,1)} copy-done((bf16[2,2,4,16,8192]{4,3,2,1,0:T(8,128)(2,1)}, bf16[2,2,4,16,8192]{4,3,2,1,0:T(8,128)(2,1)S(1)}, u32[]{:S(2)}) %copy-start.1) | copy-done | bytes 4194328
  92.4 40.5 %correlate.1 = bf16[2,76,128,256]{3,2,1,0:T(8,128)(2,1)} custom-call(s32[64]{0:T(128)} %off_ref.1, s32[3]{0:T(128)} %pad_add_fusion.chan_ref, f32[256,384]{1,0:T(8,128)} %constant.40.clone.dft_ref, bf16[80,128]{1,0:T(8,128)(2,1)} %constant.41.clone.lag_ref, bf16[256,8192]{1,0:T(8,128)(2,1)} %bitcast.5, bf16[256,8192]{1,0:T(8,128)(2,1)} %bitcast.6), custom_call_target="tpu_custom_call" | custom-call | tf_op jit(solution)/shard_map/correlate/pallas_call | solution.py:114
Async XLA Ops:
  2.7 1.0 copy-start.2
  88.5 1.9 %copy-start = (bf16[4,4,16,8192]{3,2,1,0:T(8,128)(2,1)}, bf16[4,4,16,8192]{3,2,1,0:T(8,128)(2,1)S(1)}, u32[]{:S(2)}) copy-start(bf16[4,4,16,8192]{3,2,1,0:T(8,128)(2,1)S(1)} %get-tuple-element.19) | copy-start | bytes 12582916
  90.4 2.0 %copy-start.1 = (bf16[2,2,4,16,8192]{4,3,2,1,0:T(8,128)(2,1)}, bf16[2,2,4,16,8192]{4,3,2,1,0:T(8,128)(2,1)S(1)}, u32[]{:S(2)}) copy-start(bf16[2,2,4,16,8192]{4,3,2,1,0:T(8,128)(2,1)S(1)} %get-tuple-element.20) | copy-start | bytes 12582916

commit v4 on v3

--- a/solution.py
+++ b/solution.py
@@ -15,6 +15,7 @@
 SPAN = L + LANES
 STRIDE = 132
 GROUP = 32
+LAST = (8192 - SPAN) // LANES
 ROWS = 36
 
 
@@ -37,46 +38,61 @@
     )
     lag_t = np.zeros((LAGP, BINS), np.float32)
     lag_t[:LAGS] = lag.T
-    return shifted, lag_t.astype(jnp.bfloat16)
-
-
-def compute_kernel(off_ref, chan_ref, dft_ref, lag_ref, rcv_ref, src_ref, out_ref,
-                   spec_rcv, spec_src, wide, lagged):
+    padded = np.zeros((2, L + 2 * LANES, BINS), np.float32)
+    padded[:, LANES:LANES + L] = dft.reshape(L, 2, BINS).transpose(1, 0, 2)
+    return shifted, padded, lag_t.astype(jnp.bfloat16)
+
+
+def windows(begin, end, unroll, off_ref, dft_ref, load, wide):
+    win_count = off_ref.shape[0]
+
+    @pl.loop(begin, end, unroll=unroll)
+    def _(w):
+        first = off_ref[w]
+        base = jnp.minimum(first // LANES, LAST)
+        samples = load(pl.ds(base * LANES, SPAN))
+        if dft_ref.shape[0] == L:
+            table = pltpu.roll(dft_ref[...], first - base * LANES, 1).astype(jnp.bfloat16)
+            value = lax.dot_general(table, samples, (((1,), (1,)), ((), ())),
+                                    preferred_element_type=jnp.float32)
+            values = [value[part * BINS:(part + 1) * BINS] for part in range(2)]
+        else:
+            tables_t = [dft_ref[part, pl.ds(LANES - first + base * LANES, SPAN), :].astype(jnp.bfloat16)
+                        for part in range(2)]
+            values = [lax.dot_general(table, samples, (((0,), (1,)), ((), ())),
+                                      preferred_element_type=jnp.float32) for table in tables_t]
+        for half in range(2):
+            for part in range(2):
+                wide[half, pl.ds(part * win_count + w, BINS, stride=STRIDE), :] = (
+                    values[part][:, half * LANES:(half + 1) * LANES])
+
+
+def narrow(begin, end, taps, wide, store):
+    @pl.loop(begin, end, unroll=8)
+    def _(f):
+        for half in range(2):
+            rows = wide[half, pl.ds(pl.multiple_of(f * STRIDE, 4), taps), :]
+            store(f, half, rows.astype(jnp.bfloat16))
+
+
+def compute_kernel(off_ref, ids_ref, dft_ref, lag_ref, spec_ref, src_ref, out_ref,
+                   spec_rcv, spec_src, wide, lagged, spec_sem):
     turn, group = pl.program_id(0), pl.program_id(1)
     win_count = off_ref.shape[0]
     taps = 2 * win_count
-    last = rcv_ref.shape[1] // LANES - SPAN // LANES
-
-    def spectra(records_ref, store):
-        @pl.loop(0, win_count, unroll=8)
-        def _(w):
-            first = off_ref[w]
-            base = jnp.minimum(first // LANES, last)
-            table = pltpu.roll(dft_ref[...], first - base * LANES, 1).astype(jnp.bfloat16)
-            samples = records_ref[:, pl.ds(pl.multiple_of(base * LANES, LANES), SPAN)]
-            value = lax.dot_general(table, samples, (((1,), (1,)), ((), ())),
-                                    preferred_element_type=jnp.float32)
-            for half in range(2):
-                for part in range(2):
-                    wide[half, pl.ds(part * win_count + w, BINS, stride=STRIDE), :] = (
-                        value[part * BINS:(part + 1) * BINS, half * LANES:(half + 1) * LANES])
-
-        @pl.loop(0, BINS, unroll=8)
-        def _(f):
-            for half in range(2):
-                rows = wide[half, pl.ds(pl.multiple_of(f * STRIDE, 4), taps), :]
-                store(f, half, rows.astype(jnp.bfloat16))
+    rcv_first = lax.axis_index("rcv") * spec_rcv.shape[2]
+    fetch = pltpu.make_async_copy(spec_ref, spec_rcv, spec_sem)
 
     @pl.when((turn == 0) & (group == 0))
     def _():
-        def to_rcv(f, half, rows):
-            spec_rcv[f, :, half * LANES:(half + 1) * LANES] = rows
+        fetch.start()
 
         def to_src(f, half, rows):
             spec_src[half, f] = rows
 
-        spectra(rcv_ref, to_rcv)
-        spectra(src_ref, to_src)
+        windows(0, win_count, 8, off_ref, dft_ref, lambda span: src_ref[:, span], wide)
+        narrow(0, BINS, taps, wide, to_src)
+        fetch.wait()
 
     @pl.when(group == 0)
     def _():
@@ -94,9 +110,9 @@
         value = jnp.dot(lag_ref[...], cross, preferred_element_type=jnp.float32)
         for half in range(2):
             lagged[half, pl.ds(s, LAGP, stride=ROWS), :] = value[:, half * LANES:(half + 1) * LANES]
-    src_chan = chan_ref[turn] + group * GROUP + lax.broadcasted_iota(jnp.int32, (GROUP, LANES), 0)
+    src_chan = ids_ref[turn] * SB + group * GROUP + lax.broadcasted_iota(jnp.int32, (GROUP, LANES), 0)
     for half in range(2):
-        rcv_chan = chan_ref[2] + half * LANES + lax.broadcasted_iota(jnp.int32, (GROUP, LANES), 1)
+        rcv_chan = rcv_first + half * LANES + lax.broadcasted_iota(jnp.int32, (GROUP, LANES), 1)
         apart = src_chan != rcv_chan
         for lag in range(LAGS):
             value = lagged[half, lag * ROWS:lag * ROWS + GROUP, :]
@@ -104,12 +120,10 @@
                 jnp.where(apart, value, 0.0).astype(jnp.bfloat16))
 
 
-def compute(offsets, chans, rcv, src):
+def compute(offsets, block_ids, dft, lag, spec, src):
     win_count = offsets.shape[0]
-    turns = src.shape[0] // SB
-    rcv_total = rcv.shape[0]
-    dft, lag = tables(win_count)
-    taps = 2 * win_count
+    turns = block_ids.shape[0]
+    bins, taps, rcv_total = spec.shape
     whole = lambda shape: pl.BlockSpec(shape, lambda t, g, *_: (0,) * len(shape), pipeline_mode=pl.Buffered(1))
     return pl.pallas_call(
         compute_kernel,
@@ -117,28 +131,30 @@
         grid_spec=pltpu.PrefetchScalarGridSpec(
             num_scalar_prefetch=2,
             grid=(turns, SB // GROUP),
-            in_specs=[whole(dft.shape), whole(lag.shape), whole(rcv.shape), whole(src.shape)],
+            in_specs=[whole(dft.shape), whole(lag.shape), pl.BlockSpec(memory_space=pl.ANY), whole(src.shape)],
             out_specs=pl.BlockSpec((1, LAGS, GROUP, rcv_total), lambda t, g, *_: (t, 0, g, 0)),
             scratch_shapes=[
-                pltpu.VMEM((BINS, taps, rcv_total), jnp.bfloat16),
-                pltpu.VMEM((turns, BINS, taps, SB), jnp.bfloat16),
+                pltpu.VMEM((bins, taps, rcv_total), jnp.bfloat16),
+                pltpu.VMEM((turns, bins, taps, SB), jnp.bfloat16),
                 pltpu.VMEM((2, BINS * STRIDE, LANES), jnp.float32),
                 pltpu.VMEM((2, LAGP * ROWS, LANES), jnp.float32),
+                pltpu.SemaphoreType.DMA,
             ],
         ),
         out_shape=jax.ShapeDtypeStruct((turns, LAGS, SB, rcv_total), jnp.bfloat16),
         compiler_params=pltpu.CompilerParams(vmem_limit_bytes=56 * 1024 * 1024),
-    )(offsets, chans, dft, lag, rcv, src)
+    )(offsets, block_ids, dft, lag, spec, src)
 
 
 NX, NY, NZ, NC = 4, 4, 8, 2
 ZL = NZ // 2
 PIECES = 4
-SKEW = 1
+OFFSETS = (0, 0, 0, 0)
 MESH = pl.DeviceIdType.MESH
 
 
-def gather_kernel(rec_ref, live_ref, ids_ref, rcv_ref, src_ref, *scratch):
+def gather_kernel(off_ref, live_ref, ids_ref, dft_ref, rec_ref, spec_out, src_out, rcv_ref, src_ref, spec_ref,
+                  wide, *scratch):
     columns, first, mixed, second, landed, chosen, merged = (
         scratch[i * PIECES:(i + 1) * PIECES] for i in range(7))
     (id_buf, id_smem, z_send, z_recv, c_send, c_recv, x_send, x_recv, y_send, y_recv,
@@ -179,13 +195,17 @@
     for peer in peers:
         pl.semaphore_signal(barrier, inc=1, device_id=peer, device_id_type=MESH)
 
-    live = live_ref[:, :1]
+    rows = lax.broadcasted_iota(jnp.int32, (shard, LANES), 0)
+    live = jnp.zeros((shard, LANES), jnp.float32)
+    for channel in range(shard):
+        live = jnp.where(rows == channel, live_ref[channel].astype(jnp.float32), live)
+    live = live[:, :1].astype(rec_ref.dtype)
     for t in range(PIECES):
         columns[t][core, z] = rec_ref[:, t * width:(t + 1) * width] * live
-    id_buf[y] = ids_ref[...]
+    id_buf[y] = jnp.where(lax.broadcasted_iota(jnp.int32, (8, LANES), 0) == 0, ids_ref[0], ids_ref[1])
     pl.semaphore_wait(barrier, len(peers))
 
-    ids = [send(ids_ref, id_buf.at[y], i_send.at[d - 1], i_recv.at[d - 1],
+    ids = [send(id_buf.at[y], id_buf.at[y], i_send.at[d - 1], i_recv.at[d - 1],
                 device(y_to=(y + d) % NY)) for d in range(1, NY)]
 
     def ids_ready():
@@ -195,8 +215,6 @@
         to_smem.start()
         to_smem.wait()
 
-    locals_started = []
-
     def piece(t):
         hops = (4, 3) if t % 2 == 0 else (3, 4)
         lanes = pl.ds(t * width, width)
@@ -217,6 +235,7 @@
             for way in range(2):
                 hop_send(way, 1)
             share(z, 0)
+            receivers(zl)
 
         def hop_stage(hop):
             def run():
@@ -226,20 +245,27 @@
                         if hop < hops[way]:
                             hop_send(way, hop + 1)
                         share((z - hop + NZ) % NZ if way == 0 else (z + hop) % NZ, hop + way * hops[0])
+                if hop < ZL:
+                    receivers(jnp.where(zl == ZL - 1, ZL - 1 - hop, (zl + hop) % ZL))
             return run
 
-        def receivers():
-            own = columns[t].at[core, pl.ds(zh * ZL, ZL)]
-            target = rcv_ref.at[:, y, :, lanes]
-            state["ring"] = [send(own, target, r_send.at[t, way], r_recv.at[t, way],
-                                  device(y_to=step(y, way, NY))) for way in range(2)]
-            copy = pltpu.make_async_copy(own, target, local_sem.at[1 + t])
-            copy.start()
-            locals_started.append(copy)
+        def ring_copy(way, src_ref, dst_ref):
+            return pltpu.make_async_remote_copy(
+                src_ref=src_ref, dst_ref=dst_ref, send_sem=r_send.at[t, way], recv_sem=r_recv.at[t, way],
+                device_id=device(y_to=step(y, way, NY)), device_id_type=MESH)
+
+        def receivers(member):
+            own, target = columns[t].at[core, zh * ZL + member], rcv_ref.at[member, y, :, lanes]
+            for way in range(2):
+                ring_copy(way, own, target).start()
+            pltpu.make_async_copy(own, target, local_sem.at[1 + t]).start()
+
+        def ring_whole(way):
+            return ring_copy(way, columns[t].at[core, pl.ds(zh * ZL, ZL)], rcv_ref.at[:, y, :, lanes])
 
         def receivers_on():
             way = t % 2
-            state["ring"][way].wait_recv()
+            ring_whole(way).wait_recv()
             held = rcv_ref.at[:, step(y, 1 - way, NY), :, lanes]
             state["on"] = send(held, held, r_send.at[t, 2], r_recv.at[t, 2], device(y_to=step(y, way, NY)))
 
@@ -320,35 +346,72 @@
             whole = src_ref.at[core, :, :, :, lanes]
             state["twin"] = send(whole, whole, e_send.at[t], e_recv.at[t], sibling)
 
+        def receivers_done():
+            ring_whole(1 - t % 2).wait_recv()
+            state["on"].wait_recv()
+            for way in range(2):
+                ring_whole(way).wait_send()
+            pltpu.make_async_copy(columns[t].at[core, pl.ds(zh * ZL, ZL)], rcv_ref.at[:, y, :, lanes],
+                                  local_sem.at[1 + t]).wait()
+
         def finish():
-            state["ring"][1 - t % 2].wait_recv()
-            state["on"].wait_recv()
             state["twin"].wait_recv()
+            held = src_ref.at[:, :, :, :, lanes]
+            state["out"] = pltpu.make_async_copy(held, src_out.at[:, :, :, :, lanes], local_sem.at[1 + 2 * PIECES + t])
+            state["out"].start()
+
+        def end():
+            state["out"].wait()
 
         return [begin] + [hop_stage(hop) for hop in range(1, NZ // 2 + 1)] + [
-            pick, receivers, blend, choose, receivers_on, spread, spread_on, twin, finish]
-
-    pieces = [piece(t) for t in range(PIECES)]
-    for slot in range(len(pieces[0]) + SKEW * (PIECES - 1)):
+            pick, blend, receivers_on, choose, receivers_done, spread, spread_on, twin, finish, end]
+
+    taps, count = spec_ref.shape[1], off_ref.shape[0]
+    stored = []
+
+    def to_spec(f, lane_half, values):
+        spec_ref[f, :, lane_half * LANES:(lane_half + 1) * LANES] = values
+
+    def windows_part(k, parts):
+        windows(k * count // parts, (k + 1) * count // parts, 4, off_ref, dft_ref,
+                lambda span: rcv_ref[:, :, :, span].reshape(ZL * NY * shard, SPAN), wide)
+
+    def narrow_part(k, parts):
+        size = BINS // parts
+        narrow(k * size, (k + 1) * size, taps, wide, to_spec)
+        piece_of = pl.ds(k * size, size)
+        copy = pltpu.make_async_copy(spec_ref.at[piece_of], spec_out.at[piece_of],
+                                     local_sem.at[1 + 3 * PIECES + k])
+        copy.start()
+        stored.append(copy)
+
+    stages = [piece(t) for t in range(PIECES)]
+    for slot in range(len(stages[0])):
         for t in range(PIECES):
-            if 0 <= slot - SKEW * t < len(pieces[t]):
-                pieces[t][slot - SKEW * t]()
-    for copy in locals_started:
+            stages[t][slot]()
+            late = slot - (len(stages[0]) - 5)
+            if late in (0, 1):
+                windows_part(late * PIECES + t, 2 * PIECES)
+            if late == 2:
+                narrow_part(t, PIECES)
+    for copy in stored:
         copy.wait()
     for copy in sent:
         copy.wait_send()
 
 
-def gather(records, live_mask, block_ids):
+def gather(records, live_mask, offsets, block_ids, dft):
     shard, total = records.shape
     width = total // PIECES
     part = width // NX
     half = part // 2
     turns = block_ids.shape[0]
-    live = jnp.broadcast_to(live_mask[:, None].astype(records.dtype), (shard, LANES))
-    ids = jnp.zeros((8, LANES), jnp.int32).at[:turns].set(block_ids)
+    taps = 2 * offsets.shape[0]
+    rcv_total = ZL * NY * shard
     dma = pltpu.SemaphoreType.DMA
     vmem = pl.BlockSpec(memory_space=pltpu.VMEM)
+    smem = pl.BlockSpec(memory_space=pltpu.SMEM)
+    hbm = pl.BlockSpec(memory_space=pl.ANY)
     buffers = [
         (NC, NZ, shard, width),
         (2, NY, 2, shard, half),
@@ -360,34 +423,39 @@
     ]
     counts = [(PIECES, 2, 4), (PIECES, NZ), (PIECES, 4), (PIECES, 3), (PIECES, 4), (PIECES,),
               (PIECES, 3), (NY - 1,)]
-    rcv, src = pl.pallas_call(
+    src_shape = (turns, 2, NY, shard, total)
+    spec, src = pl.pallas_call(
         gather_kernel,
         name="gather",
-        in_specs=[vmem] * 3,
-        out_specs=[vmem] * 2,
+        in_specs=[smem] * 3 + [vmem] * 2,
+        out_specs=[hbm] * 2,
         out_shape=[
-            jax.ShapeDtypeStruct((ZL, NY, shard, total), records.dtype),
-            jax.ShapeDtypeStruct((turns, 2, NY, shard, total), records.dtype),
+            jax.ShapeDtypeStruct((BINS, taps, rcv_total), records.dtype),
+            jax.ShapeDtypeStruct(src_shape, records.dtype),
         ],
         scratch_shapes=(
-            [pltpu.VMEM(shape, records.dtype) for shape in buffers for _ in range(PIECES)]
+            [
+                pltpu.VMEM((ZL, NY, shard, total), records.dtype),
+                pltpu.VMEM(src_shape, records.dtype),
+                pltpu.VMEM((BINS, taps, rcv_total), records.dtype),
+                pltpu.VMEM((2, BINS * STRIDE, LANES), jnp.float32),
+            ]
+            + [pltpu.VMEM(shape, records.dtype) for shape in buffers for _ in range(PIECES)]
             + [pltpu.VMEM((NY, 8, LANES), jnp.int32), pltpu.SMEM((NY, 8, LANES), jnp.int32)]
             + [dma(shape) for shape in counts for _ in range(2)]
-            + [dma((1 + 2 * PIECES,))]
+            + [dma((1 + 4 * PIECES,))]
         ),
         compiler_params=pltpu.CompilerParams(
-            collective_id=0, has_side_effects=True, vmem_limit_bytes=40 * 1024 * 1024),
-    )(records, live, ids)
-    return rcv.reshape(-1, total), src.reshape(-1, total)
+            collective_id=0, has_side_effects=True, vmem_limit_bytes=56 * 1024 * 1024),
+    )(offsets, live_mask, block_ids, dft, records)
+    return spec, src.reshape(-1, total)
 
 
 def local(records, live_mask, offsets, block_ids):
-    members = records.shape[0] * lax.axis_size("src")
-    rcv, src = gather(records, live_mask, block_ids)
-    first = block_ids[:, 0] * SB
-    group = lax.axis_index("rcv")
-    chans = jnp.concatenate([first, (group * members)[None].astype(jnp.int32)])
-    return compute(offsets, chans, rcv, src)
+    dft, padded, lag = tables(offsets.shape[0])
+    block_ids = block_ids.reshape(-1)
+    spec, src = gather(records, live_mask, offsets, block_ids, padded)
+    return compute(offsets, block_ids, dft, lag, spec, src)
 
 
 def solution(mesh):

time: 133 us -> 108 us (0.81)
  Pallas kernels: 125 us -> 108 us
  local copies, waits for them, and re-layouts: 5.65 us -> 0 us
  other arithmetic: 1.87 us -> 0 us
    pallas_call x1, Pallas kernels: 40.5 us -> 30.3 us  [compute(): pl.pallas_call(compute_kernel, name='correlate', grid_spec=pltpu.Prefetch...]
    pallas_call x1, Pallas kernels: 84.9 us -> 77.7 us  [gather(): pl.pallas_call(gather_kernel, name='gather', in_specs=[smem] * 3 + [vmem]...]
    unnamed x6 -> x0, local copies, waits for them, and re-layouts: 4.85 us -> none
where the time goes in v4:
time: 108 us
  Pallas kernels  108 us (100%)
    pallas_call x1, Pallas kernels, gather(): pl.pallas_call(gather_kernel, name='gather', in_specs=[smem] * 3 + [vmem]...  77.7 us
    pallas_call x1, Pallas kernels, compute(): pl.pallas_call(compute_kernel, name='correlate', grid_spec=pltpu.Prefetch...  30.3 us

profile of v4, /device:TPU:1, one launch (start us, length us, event | category | flops | bytes accessed | tf_op | source)
XLA Modules:
  0.0 108.0 jit_solution(6105963049898664918)
XLA Ops:
  0.0 77.7 %gather.1 = (bf16[128,128,256]{2,1,0:T(8,128)(2,1)}, bf16[2,2,4,16,8192]{4,3,2,1,0:T(8,128)(2,1)}) custom-call(s32[64]{0:T(128)} %off_ref.3, s32[16]{0:T(128)} %live_ref.1, s32[2]{0:T(128)} %bitcast.3, f32[2,512,128]{2,1,0:T(8,128)} %constant.6.clone.dft_ref, bf16[16,8192]{1,0:T(8,128)(2,1)} %rec_ref.1), custom_call_target="tpu_custom_call" | custom-call | tf_op jit(solution)/shard_map/gather/pallas_call | solution.py:427
  77.8 30.3 %correlate.1 = bf16[2,76,128,256]{3,2,1,0:T(8,128)(2,1)} custom-call(s32[64]{0:T(128)} %off_ref.3, s32[2]{0:T(128)} %bitcast.4, f32[256,384]{1,0:T(8,128)} %constant.7.clone.dft_ref, bf16[80,128]{1,0:T(8,128)(2,1)} %constant.8.clone.lag_ref, bf16[128,128,256]{2,1,0:T(8,128)(2,1)} %get-tuple-element.7.spec_ref, bf16[256,8192]{1,0:T(8,128)(2,1)} %bitcast.2), custom_call_target="tpu_custom_call" | custom-call | tf_op jit(solution)/shard_map/correlate/pallas_call | solution.py:128

commit v5 on v4

--- a/solution.py
+++ b/solution.py
@@ -87,18 +87,15 @@
     def _():
         fetch.start()
 
-        def to_src(f, half, rows):
-            spec_src[half, f] = rows
-
-        windows(0, win_count, 8, off_ref, dft_ref, lambda span: src_ref[:, span], wide)
-        narrow(0, BINS, taps, wide, to_src)
+        windows(0, win_count, 8, off_ref, dft_ref, lambda span: src_ref[:, span], spec_src)
         fetch.wait()
 
     @pl.when(group == 0)
     def _():
         @pl.loop(0, BINS, unroll=8)
         def _(f):
-            value = lax.dot_general(spec_src[turn, f], spec_rcv[f], (((0,), (0,)), ((), ())),
+            source = spec_src[turn, pl.ds(pl.multiple_of(f * STRIDE, 4), taps), :].astype(jnp.bfloat16)
+            value = lax.dot_general(source, spec_rcv[f], (((0,), (0,)), ((), ())),
                                     preferred_element_type=jnp.float32)
             for half in range(2):
                 wide[half, pl.ds(f, SB, stride=STRIDE), :] = value[:, half * LANES:(half + 1) * LANES]
@@ -135,14 +132,14 @@
             out_specs=pl.BlockSpec((1, LAGS, GROUP, rcv_total), lambda t, g, *_: (t, 0, g, 0)),
             scratch_shapes=[
                 pltpu.VMEM((bins, taps, rcv_total), jnp.bfloat16),
-                pltpu.VMEM((turns, bins, taps, SB), jnp.bfloat16),
+                pltpu.VMEM((turns, BINS * STRIDE, SB), jnp.float32),
                 pltpu.VMEM((2, BINS * STRIDE, LANES), jnp.float32),
                 pltpu.VMEM((2, LAGP * ROWS, LANES), jnp.float32),
                 pltpu.SemaphoreType.DMA,
             ],
         ),
         out_shape=jax.ShapeDtypeStruct((turns, LAGS, SB, rcv_total), jnp.bfloat16),
-        compiler_params=pltpu.CompilerParams(vmem_limit_bytes=56 * 1024 * 1024),
+        compiler_params=pltpu.CompilerParams(vmem_limit_bytes=60 * 1024 * 1024),
     )(offsets, block_ids, dft, lag, spec, src)
 
 
@@ -364,7 +361,7 @@
             state["out"].wait()
 
         return [begin] + [hop_stage(hop) for hop in range(1, NZ // 2 + 1)] + [
-            pick, blend, receivers_on, choose, receivers_done, spread, spread_on, twin, finish, end]
+            pick, receivers_on, blend, choose, receivers_done, spread, spread_on, twin, finish, end]
 
     taps, count = spec_ref.shape[1], off_ref.shape[0]
     stored = []

time: 108 us -> 105 us (0.972)
  Pallas kernels: 108 us -> 105 us
    pallas_call x1, Pallas kernels: 77.7 us -> 75.6 us  [gather(): pl.pallas_call(gather_kernel, name='gather', in_specs=[smem] * 3 + [vmem]...]
where the time goes in v5:
time: 105 us
  Pallas kernels  105 us (100%)
    pallas_call x1, Pallas kernels, gather(): pl.pallas_call(gather_kernel, name='gather', in_specs=[smem] * 3 + [vmem]...  75.6 us
    pallas_call x1, Pallas kernels, compute(): pl.pallas_call(compute_kernel, name='correlate', grid_spec=pltpu.Prefetch...  29.4 us

profile of v5, /device:TPU:1, one launch (start us, length us, event | category | flops | bytes accessed | tf_op | source)
XLA Modules:
  0.0 105.1 jit_solution(2541034203948593509)
XLA Ops:
  0.0 75.6 %gather.1 = (bf16[128,128,256]{2,1,0:T(8,128)(2,1)}, bf16[2,2,4,16,8192]{4,3,2,1,0:T(8,128)(2,1)}) custom-call(s32[64]{0:T(128)} %off_ref.3, s32[16]{0:T(128)} %live_ref.1, s32[2]{0:T(128)} %bitcast.3, f32[2,512,128]{2,1,0:T(8,128)} %constant.6.clone.dft_ref, bf16[16,8192]{1,0:T(8,128)(2,1)} %rec_ref.1), custom_call_target="tpu_custom_call" | custom-call | tf_op jit(solution)/shard_map/gather/pallas_call | solution.py:424
  75.6 29.4 %correlate.1 = bf16[2,76,128,256]{3,2,1,0:T(8,128)(2,1)} custom-call(s32[64]{0:T(128)} %off_ref.3, s32[2]{0:T(128)} %bitcast.4, f32[256,384]{1,0:T(8,128)} %constant.7.clone.dft_ref, bf16[80,128]{1,0:T(8,128)(2,1)} %constant.8.clone.lag_ref, bf16[128,128,256]{2,1,0:T(8,128)(2,1)} %get-tuple-element.7.spec_ref, bf16[256,8192]{1,0:T(8,128)(2,1)} %bitcast.2), custom_call_target="tpu_custom_call" | custom-call | tf_op jit(solution)/shard_map/correlate/pallas_call | solution.py:125

commit v6 on v5

--- a/solution.py
+++ b/solution.py
@@ -14,9 +14,9 @@
 LANES = 128
 SPAN = L + LANES
 STRIDE = 132
-GROUP = 32
+GROUP = 64
 LAST = (8192 - SPAN) // LANES
-ROWS = 36
+ROWS = 68
 
 
 def tables(win_count):
@@ -87,12 +87,12 @@
     def _():
         fetch.start()
 
-        windows(0, win_count, 8, off_ref, dft_ref, lambda span: src_ref[:, span], spec_src)
+        windows(0, win_count, 16, off_ref, dft_ref, lambda span: src_ref[:, span], spec_src)
         fetch.wait()
 
     @pl.when(group == 0)
     def _():
-        @pl.loop(0, BINS, unroll=8)
+        @pl.loop(0, BINS, unroll=32)
         def _(f):
             source = spec_src[turn, pl.ds(pl.multiple_of(f * STRIDE, 4), taps), :].astype(jnp.bfloat16)
             value = lax.dot_general(source, spec_rcv[f], (((0,), (0,)), ((), ())),

time: 105 us -> 99.5 us (0.948)
  Pallas kernels: 105 us -> 99.3 us
    pallas_call x1, Pallas kernels: 29.4 us -> 23.7 us  [compute(): pl.pallas_call(compute_kernel, name='correlate', grid_spec=pltpu.Prefetch...]
where the time goes in v6:
time: 99.5 us; the launch traced here: 99.3 us
  Pallas kernels  99.3 us (100%)
    pallas_call x1, Pallas kernels, gather(): pl.pallas_call(gather_kernel, name='gather', in_specs=[smem] * 3 + [vmem]...  75.6 us
    pallas_call x1, Pallas kernels, compute(): pl.pallas_call(compute_kernel, name='correlate', grid_spec=pltpu.Prefetch...  23.7 us

profile of v6, /device:TPU:1, one launch (start us, length us, event | category | flops | bytes accessed | tf_op | source)
XLA Modules:
  0.0 99.3 jit_solution(1835356817601973108)
XLA Ops:
  0.0 75.6 %gather.1 = (bf16[128,128,256]{2,1,0:T(8,128)(2,1)}, bf16[2,2,4,16,8192]{4,3,2,1,0:T(8,128)(2,1)}) custom-call(s32[64]{0:T(128)} %off_ref.3, s32[16]{0:T(128)} %live_ref.1, s32[2]{0:T(128)} %bitcast.3, f32[2,512,128]{2,1,0:T(8,128)} %constant.6.clone.dft_ref, bf16[16,8192]{1,0:T(8,128)(2,1)} %rec_ref.1), custom_call_target="tpu_custom_call" | custom-call | tf_op jit(solution)/shard_map/gather/pallas_call | solution.py:424
  75.7 23.7 %correlate.1 = bf16[2,76,128,256]{3,2,1,0:T(8,128)(2,1)} custom-call(s32[64]{0:T(128)} %off_ref.3, s32[2]{0:T(128)} %bitcast.4, f32[256,384]{1,0:T(8,128)} %constant.7.clone.dft_ref, bf16[80,128]{1,0:T(8,128)(2,1)} %constant.8.clone.lag_ref, bf16[128,128,256]{2,1,0:T(8,128)(2,1)} %get-tuple-element.7.spec_ref, bf16[256,8192]{1,0:T(8,128)(2,1)} %bitcast.2), custom_call_target="tpu_custom_call" | custom-call | tf_op jit(solution)/shard_map/correlate/pallas_call | solution.py:125

commit v7 on v6

--- a/solution.py
+++ b/solution.py
@@ -92,7 +92,7 @@
 
     @pl.when(group == 0)
     def _():
-        @pl.loop(0, BINS, unroll=32)
+        @pl.loop(0, BINS, unroll=64)
         def _(f):
             source = spec_src[turn, pl.ds(pl.multiple_of(f * STRIDE, 4), taps), :].astype(jnp.bfloat16)
             value = lax.dot_general(source, spec_rcv[f], (((0,), (0,)), ((), ())),

time: 99.5 us -> 98.7 us (level)
  no operation moved by 1% of the time
where the time goes in v7:
time: 98.7 us; the launch traced here: 98.6 us
  Pallas kernels  98.6 us (100%)
    pallas_call x1, Pallas kernels, gather(): pl.pallas_call(gather_kernel, name='gather', in_specs=[smem] * 3 + [vmem]...  75.6 us
    pallas_call x1, Pallas kernels, compute(): pl.pallas_call(compute_kernel, name='correlate', grid_spec=pltpu.Prefetch...  22.9 us

profile of v7, /device:TPU:1, one launch (start us, length us, event | category | flops | bytes accessed | tf_op | source)
XLA Modules:
  0.0 98.6 jit_solution(16965250132350765097)
XLA Ops:
  0.0 75.6 %gather.1 = (bf16[128,128,256]{2,1,0:T(8,128)(2,1)}, bf16[2,2,4,16,8192]{4,3,2,1,0:T(8,128)(2,1)}) custom-call(s32[64]{0:T(128)} %off_ref.3, s32[16]{0:T(128)} %live_ref.1, s32[2]{0:T(128)} %bitcast.3, f32[2,512,128]{2,1,0:T(8,128)} %constant.6.clone.dft_ref, bf16[16,8192]{1,0:T(8,128)(2,1)} %rec_ref.1), custom_call_target="tpu_custom_call" | custom-call | tf_op jit(solution)/shard_map/gather/pallas_call | solution.py:424
  75.6 22.9 %correlate.1 = bf16[2,76,128,256]{3,2,1,0:T(8,128)(2,1)} custom-call(s32[64]{0:T(128)} %off_ref.3, s32[2]{0:T(128)} %bitcast.4, f32[256,384]{1,0:T(8,128)} %constant.7.clone.dft_ref, bf16[80,128]{1,0:T(8,128)(2,1)} %constant.8.clone.lag_ref, bf16[128,128,256]{2,1,0:T(8,128)(2,1)} %get-tuple-element.7.spec_ref, bf16[256,8192]{1,0:T(8,128)(2,1)} %bitcast.2), custom_call_target="tpu_custom_call" | custom-call | tf_op jit(solution)/shard_map/correlate/pallas_call | solution.py:125
